TPU v7x, 512 devices: a whole 4x8x8 slice. The times are simulated.
512 devices in a mesh: ctx: 256 (over z, y, x), hid: 2 (over core).
Axes of the slice: x: 4, y: 8, z: 8, core: 2. Of those that a mesh axis runs over, the one named last changes fastest.
Arguments:
- queries: bfloat16 [65536, 4096], P('ctx', 'hid'), may hold values from -8 to 8
- keys: bfloat16 [65536, 1024], P('ctx', 'hid'), may hold values from -5 to 5
- values: bfloat16 [65536, 1024], P('ctx', 'hid'), may hold values from -6 to 6
- residual: bfloat16 [65536, 4096], P('ctx', 'hid'), may hold values from -6 to 6
- out_weight: bfloat16 [4096, 4096], P('hid'), may hold values from -0.125 to 0.125
Outputs:
- layer_out: bfloat16 [65536, 4096], P('ctx', 'hid')
All inputs are finite; a program needn't handle non-finite values.
Results may differ from a plain program's by a relative error of at most 0.0044.
Values may be sent and summed in bfloat16 or wider, within the bound.
No kernel may reach another device: no remote copies, remote signals or barrier semaphores. Data moves between devices by JAX's collectives and lax.ppermute only.
A program may use at most 64 MiB of HBM per device.

v0:
```python
import math

import jax
import jax.numpy as jnp
from jax import lax
from jax.sharding import PartitionSpec as P

HEAD_SIZE = 128


def passed_along(block, axis, distance):
    devices = range(lax.axis_size(axis))
    route = [(i - distance, i) for i in devices if i - distance in devices]
    return lax.ppermute(block, axis, route)


def split_up(x, dim, devices):
    shape = x.shape
    tiles = x.reshape(*shape[:dim], devices, shape[dim] // devices, *shape[dim + 1 :])
    return jnp.moveaxis(tiles, dim, 0)


def sent_and_summed(x, axis, dim):
    devices = lax.axis_size(axis)
    tiles = lax.all_to_all(split_up(x, dim, devices), axis, 0, 0, tiled=True)
    return jnp.sum(tiles.astype(jnp.float32), axis=0)


def block_mask(local_rows, position):
    row_ids = lax.broadcasted_iota(jnp.int32, (local_rows, 5 * local_rows), 0)
    col_ids = lax.broadcasted_iota(jnp.int32, (local_rows, 5 * local_rows), 1)
    block_ids = col_ids // local_rows
    offset = col_ids - block_ids * local_rows
    distance = jnp.where(
        block_ids == 0, 0, jnp.left_shift(jnp.int32(1), jnp.maximum(block_ids - 1, 0))
    )
    return jnp.where(block_ids == 0, offset <= row_ids, position >= distance)


def attend(queries, gathered_rows, position):
    local_rows = queries.shape[0]
    kv_heads = gathered_rows.shape[2] // HEAD_SIZE
    queries_per_group = queries.shape[1] // HEAD_SIZE // kv_heads
    reshaped_output = queries.reshape(local_rows, kv_heads, queries_per_group, HEAD_SIZE)
    key_matrix = gathered_rows[0].reshape(-1, kv_heads, HEAD_SIZE)
    value_matrix = gathered_rows[1].reshape(-1, kv_heads, HEAD_SIZE)
    scores = jnp.einsum(
        "qkgd,skd->kgqs", reshaped_output, key_matrix, preferred_element_type=jnp.float32
    ) / math.sqrt(HEAD_SIZE)
    scores = jnp.where(block_mask(local_rows, position), scores, -1e30)
    row_peak = jnp.max(scores, axis=-1, keepdims=True)
    raised = jnp.exp(scores - row_peak)
    weights = (raised / jnp.sum(raised, axis=-1, keepdims=True)).astype(jnp.bfloat16)
    mixed = jnp.einsum("kgqs,skd->qkgd", weights, value_matrix, preferred_element_type=jnp.float32)
    return mixed.reshape(local_rows, -1).astype(jnp.bfloat16)


def on_device(queries, keys, values, residual, out_weight):
    position = lax.axis_index("ctx")
    stacked = jnp.stack([keys, values])
    pieces = []
    for distance in (1, 2, 4, 8):
        pieces.append(passed_along(stacked, "ctx", distance))
    gathered_rows = jnp.concatenate([stacked] + pieces, axis=1)
    attended = attend(queries, gathered_rows, position)
    summed = sent_and_summed(
        lax.dot_general(
            out_weight, attended, (((0,), (1,)), ((), ())), preferred_element_type=jnp.float32
        ).astype(jnp.bfloat16),
        "hid",
        0,
    )
    return (residual.astype(jnp.float32) + summed.T).astype(jnp.bfloat16)


def solution(mesh):
    return jax.shard_map(
        on_device,
        mesh=mesh,
        in_specs=(
            P("ctx", "hid"),
            P("ctx", "hid"),
            P("ctx", "hid"),
            P("ctx", "hid"),
            P("hid", None),
        ),
        out_specs=P("ctx", "hid"),
        check_vma=False,
    )
```

profile of v0, /device:TPU:391, one launch (start us, length us, event | category | flops | bytes accessed | tf_op | source)
XLA Modules:
  0.0 113.0 jit_solution(15711509434493806704)
XLA Ops:
  0.0 1.1 copy.14
  1.1 1.1 copy.15
  2.2 0.9 pad_maximum_fusion
  3.0 3.1 %collective-permute-start = (bf16[2,256,512]{1,2,0:T(8,128)(2,1)}, bf16[2,256,512]{1,2,0:T(8,128)(2,1)}, u32[]{:S(2)}, u32[]{:S(2)}) collective-permute-start(bf16[2,256,512]{1,2,0:T(8,128)(2,1)} %get-tuple-element.7), channel_id=1, source_target_pairs={{0,2},{2,4},{4,6},{6,8},{8,10},{10,12},{12,14},{14,16},{16,18},{18... | collective-permute-start | bytes 1572872 | tf_op jit(solution)/shard_map/ppermute | solution.py:14
  6.2 4.0 %collective-permute-start.1 = (bf16[2,256,512]{1,2,0:T(8,128)(2,1)}, bf16[2,256,512]{1,2,0:T(8,128)(2,1)}, u32[]{:S(2)}, u32[]{:S(2)}) collective-permute-start(bf16[2,256,512]{1,2,0:T(8,128)(2,1)} %get-tuple-element.7), channel_id=1, source_target_pairs={{0,4},{2,6},{4,8},{6,10},{8,12},{10,14},{12,16},{14,18},{16,20},{1... | collective-permute-start | bytes 1572872 | tf_op jit(solution)/shard_map/ppermute | solution.py:14
  10.2 3.2 %collective-permute-start.2 = (bf16[2,256,512]{1,2,0:T(8,128)(2,1)}, bf16[2,256,512]{1,2,0:T(8,128)(2,1)}, u32[]{:S(2)}, u32[]{:S(2)}) collective-permute-start(bf16[2,256,512]{1,2,0:T(8,128)(2,1)} %get-tuple-element.7), channel_id=1, source_target_pairs={{0,8},{2,10},{4,12},{6,14},{8,16},{10,18},{12,20},{14,22},{16,24},... | collective-permute-start | bytes 1572872 | tf_op jit(solution)/shard_map/ppermute | solution.py:14
  13.4 5.4 %collective-permute-start.3 = (bf16[2,256,512]{1,2,0:T(8,128)(2,1)}, bf16[2,256,512]{1,2,0:T(8,128)(2,1)S(1)}, u32[]{:S(2)}, u32[]{:S(2)}) collective-permute-start(bf16[2,256,512]{1,2,0:T(8,128)(2,1)} %get-tuple-element.7), channel_id=1, source_target_pairs={{0,16},{2,18},{4,20},{6,22},{8,24},{10,26},{12,28},{14,30},{16,32}... | collective-permute-start | bytes 1572872 | tf_op jit(solution)/shard_map/ppermute | solution.py:14
  18.9 2.1 %fusion.5 = pred[256,1280]{0,1:T(8,128)(4,1)} fusion(s32[]{:T(128)S(6)} %axis_index.15, s32[1280]{0:T(1024)S(1)} %get-tuple-element.9, s32[1280]{0:T(1024)S(1)} %get-tuple-element.10, pred[1280]{0:T(1024)(128)(4,1)S(1)} %fusion.23), kind=kLoop, calls=%fused_computation.15 | loop fusion | flops 3604480 | bytes 339204 | tf_op jit(solution)/shard_map/jit(_where)/select_n | solution.py:37
  20.9 2.6 %reshape.10 = bf16[256,4,4,128]{3,2,1,0:T(4,128)(2,1)} reshape(bf16[256,2048]{1,0:T(8,128)(2,1)} %param.5) | data formatting | bytes 2097152 | tf_op jit(solution)/shard_map/reshape | solution.py:44
  23.5 0.5 collective-permute-done
  24.0 1.1 constant_dynamic-update-slice_fusion.3
  25.1 10.2 %collective-permute-done.1 = bf16[2,256,512]{1,2,0:T(8,128)(2,1)} collective-permute-done((bf16[2,256,512]{1,2,0:T(8,128)(2,1)}, bf16[2,256,512]{1,2,0:T(8,128)(2,1)}, u32[]{:S(2)}, u32[]{:S(2)}) %collective-permute-start.1) | collective-permute-done | bytes 524320 | tf_op jit(solution)/shard_map/ppermute | solution.py:14
  35.3 1.1 constant_dynamic-update-slice_fusion.2
  36.4 12.3 %collective-permute-done.2 = bf16[2,256,512]{1,2,0:T(8,128)(2,1)} collective-permute-done((bf16[2,256,512]{1,2,0:T(8,128)(2,1)}, bf16[2,256,512]{1,2,0:T(8,128)(2,1)}, u32[]{:S(2)}, u32[]{:S(2)}) %collective-permute-start.2) | collective-permute-done | bytes 524320 | tf_op jit(solution)/shard_map/ppermute | solution.py:14
  48.8 1.1 constant_dynamic-update-slice_fusion.1
  49.8 22.9 %collective-permute-done.3 = bf16[2,256,512]{1,2,0:T(8,128)(2,1)S(1)} collective-permute-done((bf16[2,256,512]{1,2,0:T(8,128)(2,1)}, bf16[2,256,512]{1,2,0:T(8,128)(2,1)S(1)}, u32[]{:S(2)}, u32[]{:S(2)}) %collective-permute-start.3) | collective-permute-done | bytes 524320 | tf_op jit(solution)/shard_map/ppermute | solution.py:14
  72.8 1.7 %fusion.31 = (bf16[1,1280,512]{1,2,0:T(8,128)(2,1)}, bf16[1,1280,512]{1,2,0:T(8,128)(2,1)}) fusion(bf16[2,1280,512]{1,2,0:T(8,128)(2,1)S(1)} %constant_dynamic-update-slice_fusion), kind=kLoop, calls=%fused_computation.44 | loop fusion | bytes 5242880 | tf_op jit(solution)/shard_map/slice | solution.py:45
  74.4 0.0 copy-start
  74.4 0.0 copy-start.1
  74.4 9.1 %exponential_reduce_fusion = f32[4,4,256]{2,1,0:T(4,128)S(1)} fusion(bf16[1280,4,128,1]{0,2,3,1:T(8,128)(2,1)} %bitcast.44, pred[256,1280]{0,1:T(8,128)(4,1)} %fusion.5, bf16[256,4,4,128]{3,2,1,0:T(4,128)(2,1)} %reshape.10), kind=kOutput, calls=%fused_computation.4 | convolution fusion | flops 1363150080 | bytes 2703360 | tf_op jit(solution)/shard_map/sub | solution.py:52
  83.5 0.0 copy-done
  83.5 0.0 copy-done.1
  83.5 11.6 %fusion.4 = bf16[4,128,4,256]{3,1,2,0:T(8,128)(2,1)S(1)} fusion(bf16[1280,4,128,1]{0,2,3,1:T(8,128)(2,1)S(1)} %bitcast.46, f32[4,4,256]{2,1,0:T(4,128)S(1)} %exponential_reduce_fusion, bf16[1280,4,128,1]{0,2,3,1:T(8,128)(2,1)} %bitcast.45, pred[256,1280]{0,1:T(8,128)(4,1)} %fusion.5, bf16[256,4,4,128]{3,2,1,0:T(4,128)(2,1)S(1)} %copy-done.1), kind=kOutput, calls=%fused_computation.14 | convolution fusion | flops 2711098624 | bytes 5062656 | tf_op jit(solution)/shard_map/kgqs,skd->qkgd/dot_general | solution.py:54
  95.1 8.7 %convolution_convert_fusion = bf16[256,4096]{1,0:T(8,128)(2,1)S(1)} fusion(bf16[256,2048]{0,1:T(8,128)(2,1)S(1)} %bitcast.43, bf16[2048,4096]{1,0:T(8,128)(2,1)} %param.9), kind=kOutput, calls=%fused_computation.6 | convolution fusion | flops 4296015872 | bytes 19922944 | tf_op jit(solution)/shard_map/dot_general | solution.py:67
  103.8 0.1 copy.40
  103.9 6.6 %all_to_all.5 = bf16[2,2048,256]{1,2,0:T(8,128)(2,1)S(1)} all-to-all(bf16[2,2048,256]{1,2,0:T(8,128)(2,1)S(1)} %bitcast.42), channel_id=1, replica_groups=mesh['ctx'=256,'hid'=2] {'hid'}, dimensions={0} | all-to-all | bytes 4194304 | tf_op jit(solution)/shard_map/all_to_all | solution.py:25
  110.5 0.0 copy-start.2
  110.5 0.4 convert_reduce_fusion
  111.0 0.8 copy-done.2
  111.7 1.3 %fusion.3 = bf16[256,2048]{1,0:T(8,128)(2,1)} fusion(f32[2048,256]{0,1:T(8,128)S(1)} %convert_reduce_fusion, bf16[256,2048]{1,0:T(8,128)(2,1)S(1)} %copy-done.2), kind=kLoop, calls=%fused_computation.13 | loop fusion | flops 1572864 | bytes 4194304 | tf_op jit(solution)/shard_map/convert_element_type | solution.py:73
  (3 shorter events, 0.0 us)
Async XLA Ops:
  3.0 21.0 %collective-permute-start = (bf16[2,256,512]{1,2,0:T(8,128)(2,1)}, bf16[2,256,512]{1,2,0:T(8,128)(2,1)}, u32[]{:S(2)}, u32[]{:S(2)}) collective-permute-start(bf16[2,256,512]{1,2,0:T(8,128)(2,1)} %get-tuple-element.7), channel_id=1, source_target_pairs={{0,2},{2,4},{4,6},{6,8},{8,10},{10,12},{12,14},{14,16},{16,18},{18... | collective-permute-start | bytes 1572872 | tf_op jit(solution)/shard_map/ppermute | solution.py:14
  6.2 29.2 %collective-permute-start.1 = (bf16[2,256,512]{1,2,0:T(8,128)(2,1)}, bf16[2,256,512]{1,2,0:T(8,128)(2,1)}, u32[]{:S(2)}, u32[]{:S(2)}) collective-permute-start(bf16[2,256,512]{1,2,0:T(8,128)(2,1)} %get-tuple-element.7), channel_id=1, source_target_pairs={{0,4},{2,6},{4,8},{6,10},{8,12},{10,14},{12,16},{14,18},{16,20},{1... | collective-permute-start | bytes 1572872 | tf_op jit(solution)/shard_map/ppermute | solution.py:14
  10.2 38.5 %collective-permute-start.2 = (bf16[2,256,512]{1,2,0:T(8,128)(2,1)}, bf16[2,256,512]{1,2,0:T(8,128)(2,1)}, u32[]{:S(2)}, u32[]{:S(2)}) collective-permute-start(bf16[2,256,512]{1,2,0:T(8,128)(2,1)} %get-tuple-element.7), channel_id=1, source_target_pairs={{0,8},{2,10},{4,12},{6,14},{8,16},{10,18},{12,20},{14,22},{16,24},... | collective-permute-start | bytes 1572872 | tf_op jit(solution)/shard_map/ppermute | solution.py:14
  13.4 59.3 %collective-permute-start.3 = (bf16[2,256,512]{1,2,0:T(8,128)(2,1)}, bf16[2,256,512]{1,2,0:T(8,128)(2,1)S(1)}, u32[]{:S(2)}, u32[]{:S(2)}) collective-permute-start(bf16[2,256,512]{1,2,0:T(8,128)(2,1)} %get-tuple-element.7), channel_id=1, source_target_pairs={{0,16},{2,18},{4,20},{6,22},{8,24},{10,26},{12,28},{14,30},{16,32}... | collective-permute-start | bytes 1572872 | tf_op jit(solution)/shard_map/ppermute | solution.py:14
  74.4 9.1 %copy-start = (bf16[1,1280,512]{1,2,0:T(8,128)(2,1)S(1)}, bf16[1,1280,512]{1,2,0:T(8,128)(2,1)}, u32[]{:S(2)}) copy-start(bf16[1,1280,512]{1,2,0:T(8,128)(2,1)} %get-tuple-element.6) | copy-start | bytes 3932164
  74.4 9.1 %copy-start.1 = (bf16[256,4,4,128]{3,2,1,0:T(4,128)(2,1)S(1)}, bf16[256,4,4,128]{3,2,1,0:T(4,128)(2,1)}, u32[]{:S(2)}) copy-start(bf16[256,4,4,128]{3,2,1,0:T(4,128)(2,1)} %reshape.10) | copy-start | bytes 3145732
  110.5 1.2 %copy-start.2 = (bf16[256,2048]{1,0:T(8,128)(2,1)S(1)}, bf16[256,2048]{1,0:T(8,128)(2,1)}, u32[]{:S(2)}) copy-start(bf16[256,2048]{1,0:T(8,128)(2,1)} %param.8) | copy-start | bytes 3145732
where the time goes:
time: 113 us
  waiting for transfers between devices  46 us (41%)
  matrix products  29.3 us (26%)
  starting transfers between devices  15.8 us (14%)
  local copies, waits for them, and re-layouts  10.6 us (9%)
  blocking collectives  6.59 us (6%)
  other arithmetic  4.64 us (4%)
    ppermute x4, waiting for transfers between devices, passed_along(): return lax.ppermute(block, axis, route)  46 us
    ppermute x4, starting transfers between devices, passed_along(): return lax.ppermute(block, axis, route)  15.8 us
    dot_general x1, matrix products, attend(): jnp.einsum('kgqs,skd->qkgd', weights, value_matrix, preferred_element_typ...  11.6 us
    sub x1, matrix products, attend(): raised = jnp.exp(scores - row_peak)  9.07 us
    dot_general x1, matrix products, on_device(): lax.dot_general(out_weight, attended, (((0,), (1,)), ((), ())), preferred...  8.66 us
    all_to_all x1, blocking collectives, sent_and_summed(): tiles = lax.all_to_all(split_up(x, dim, devices), axis, 0, 0, tiled=True)  6.59 us
    unnamed x11, local copies, waits for them, and re-layouts  6.17 us
    reshape x1, local copies, waits for them, and re-layouts, attend(): queries.reshape(local_rows, kv_heads, queries_per_group, HEAD_SIZE)  2.56 us
  transfers between devices with their start and end apart: 4, of which 4 were waited for; matrix products, arithmetic and copies ran while one was open for 7% of the time, Pallas kernels for 0%

commit v1 on v0

v1 whole, which is shorter than its diff:
```python
import functools
import math

import jax
import jax.numpy as jnp
from jax import lax
from jax.experimental import pallas as pl
from jax.experimental.pallas import tpu as pltpu
from jax.sharding import PartitionSpec as P


HEAD = 128
SCALE = math.log2(math.e) / math.sqrt(HEAD)
MIB = 1 << 20
F32, BF16 = jnp.float32, jnp.bfloat16


def route(axis, target):
    n = lax.axis_size(axis)
    return [(i, target(i)) for i in range(n) if target(i) is not None and 0 <= target(i) < n]


def head_step(q, blocks, prev, group, rows):
    tile = 128
    ones = jnp.ones((rows, HEAD), BF16)
    wide = [jnp.concatenate([v, ones], axis=1) for _, v, _, _ in blocks]
    units = [(j, r) for j in range(group) for r in range(0, rows, tile)]

    def seen(kind, r):
        return r + tile if kind == "own" else rows

    def scores_of(unit):
        j, r = unit
        qj = q[r : r + tile, j * HEAD : (j + 1) * HEAD]
        out = []
        for k, _, kind, _ in blocks:
            n = seen(kind, r)
            s = lax.dot_general(qj, k[:n], (((1,), (1,)), ((), ())), preferred_element_type=F32)
            if kind == "own":
                row = lax.broadcasted_iota(jnp.int32, (tile, n), 0) + r
                s = jnp.where(lax.broadcasted_iota(jnp.int32, (tile, n), 1) <= row, s, -1e30)
            out.append(s)
        return out

    ahead = scores_of(units[0])
    for i, (j, r) in enumerate(units):
        scores = ahead
        if True and i + 1 < len(units):
            ahead = scores_of(units[i + 1])
        tops = []
        for s, (_, _, kind, valid) in zip(scores, blocks):
            top = s[:, :HEAD]
            for t in range(HEAD, s.shape[1], HEAD):
                top = jnp.maximum(top, s[:, t : t + HEAD])
            tops.append(top if kind == "own" else jnp.where(valid, top, -1e30))
        top = functools.reduce(jnp.maximum, tops)
        m = jnp.broadcast_to(jnp.max(top, axis=1, keepdims=True), top.shape)
        if prev is not None:
            acc0, m0, l0 = prev(j, pl.ds(r, tile))
            m = jnp.maximum(m, m0)
        mc = m * SCALE
        total = None
        for s, w, (_, _, kind, valid) in zip(scores, wide, blocks):
            shift = mc if kind == "own" else jnp.where(valid, mc, 1e30)
            n = s.shape[1]
            p = jnp.exp2(s * SCALE - jnp.concatenate([shift] * (n // HEAD), axis=1)).astype(BF16)
            part = jnp.dot(p, w[:n], preferred_element_type=F32)
            total = part if total is None else total + part
        acc, l = total[:, :HEAD], total[:, HEAD:]
        if prev is not None:
            alpha = jnp.exp2(m0 * SCALE - mc)
            acc = acc + alpha * acc0
            l = l + alpha * l0
        yield j, pl.ds(r, tile), (acc, m, l)
        if not True and i + 1 < len(units):
            ahead = scores_of(units[i + 1])


def columns(start, size):
    return pl.ds(pl.multiple_of(start, HEAD), size)


def reader(state):
    return lambda j, r: tuple(ref[r, j * HEAD : (j + 1) * HEAD] for ref in state)


def part_kernel(distances, has_prev, fetch, *refs):
    refs = list(refs)
    q_ref = refs.pop(0)
    pairs = [(refs.pop(0), refs.pop(0)) for _ in distances]
    prev_refs = [refs.pop(0) for _ in range(3)] if has_prev else None
    w_hbm = refs.pop(0) if fetch else None
    state = [refs.pop(0) for _ in range(3)]
    w_vmem = refs.pop(0) if fetch else None
    g = pl.program_id(0)
    rows = q_ref.shape[0]
    group = q_ref.shape[1] // HEAD
    if fetch:
        copy = pltpu.make_async_copy(w_hbm, w_vmem, refs.pop(0))
        pl.when(g == 0)(copy.start)
    position = lax.axis_index("ctx")
    blocks = [
        (k[...], v[...], "own" if d == 0 else "far", position >= d)
        for (k, v), d in zip(pairs, distances)
    ]
    prev = reader(prev_refs) if has_prev else None
    for j, r, new in head_step(q_ref[...], blocks, prev, group, rows):
        for ref, value in zip(state, new):
            ref[r, j * HEAD : (j + 1) * HEAD] = value
    if fetch:
        pl.when(g == pl.num_programs(0) - 1)(copy.wait)


def last_kernel(distances, q_ref, *refs):
    refs = list(refs)
    pairs = [(refs.pop(0), refs.pop(0)) for _ in distances]
    *state, att_ref = refs
    rows = q_ref.shape[0]
    group = q_ref.shape[1] // HEAD
    position = lax.axis_index("ctx")
    blocks = [(k[...], v[...], "far", position >= d) for (k, v), d in zip(pairs, distances)]
    for j, r, (acc, _, l) in head_step(q_ref[...], blocks, reader(state), group, rows):
        att_ref[r, j * HEAD : (j + 1) * HEAD] = (acc / l).astype(BF16)


def partner_kernel(att_ref, w_ref, send_ref):
    width = send_ref.shape[1]
    base = (1 - lax.axis_index("hid")) * width
    tile = 512

    @pl.loop(0, width // tile)
    def _(t):
        send_ref[:, columns(t * tile, tile)] = jnp.dot(
            att_ref[...], w_ref[:, columns(base + t * tile, tile)], preferred_element_type=F32
        ).astype(BF16)


def own_kernel(att_ref, w_ref, res_ref, out_ref):
    width = out_ref.shape[1]
    base = lax.axis_index("hid") * width
    tile = 512

    @pl.loop(0, width // tile)
    def _(t):
        here = columns(t * tile, tile)
        out_ref[:, here] = res_ref[:, here].astype(F32) + jnp.dot(
            att_ref[...], w_ref[:, columns(base + t * tile, tile)], preferred_element_type=F32
        )


def pack_kernel(a_ref, b_ref, out_ref, sems):
    rows = a_ref.shape[0]
    copies = [
        pltpu.make_async_copy(ref, out_ref.at[pl.ds(i * rows, rows)], sems.at[i])
        for i, ref in enumerate((a_ref, b_ref))
    ]
    for c in copies:
        c.start()
    for c in copies:
        c.wait()


def choose_kernel(both_ref, back_ref, two_ref, one_ref):
    rows = one_ref.shape[0]
    column = lax.rem(lax.axis_index("ctx"), 4)

    @pl.when(column < 2)
    def _():
        two_ref[...] = both_ref[...]

    @pl.when(column >= 2)
    def _():
        two_ref[...] = back_ref[...]

    @pl.when(column < 3)
    def _():
        one_ref[...] = both_ref[rows:]

    @pl.when(column == 3)
    def _():
        one_ref[...] = back_ref[rows:]


WHOLE = pl.BlockSpec(memory_space=pltpu.VMEM)
ANY = pl.BlockSpec(memory_space=pltpu.HBM)


def kv_specs(source, rows):
    if isinstance(source, tuple):
        return list(source), [pl.BlockSpec((rows, HEAD), lambda g: (0, g))] * 2
    return [source, source], [
        pl.BlockSpec((rows, HEAD), lambda g: (0, g)),
        pl.BlockSpec((rows, HEAD), lambda g: (1, g)),
    ]


def packed(keys, values):
    rows, width = keys.shape
    return pl.pallas_call(
        pack_kernel,
        out_shape=pltpu.VMEM((2 * rows, width), keys.dtype),
        in_specs=[ANY, ANY],
        out_specs=WHOLE,
        scratch_shapes=[pltpu.SemaphoreType.DMA((2,))],
        compiler_params=pltpu.CompilerParams(vmem_limit_bytes=4 * MIB),
    )(*(pltpu.with_memory_space_constraint(a, pltpu.HBM) for a in (keys, values)))


def chosen(both, back):
    rows, width = both.shape
    return pl.pallas_call(
        choose_kernel,
        out_shape=(pltpu.VMEM(both.shape, both.dtype), pltpu.VMEM((rows // 2, width), both.dtype)),
        in_specs=[WHOLE, WHOLE],
        out_specs=(WHOLE, WHOLE),
        compiler_params=pltpu.CompilerParams(vmem_limit_bytes=4 * MIB),
    )(both, back)


def cost(rows, width, blocks, extra=0):
    return pl.CostEstimate(
        flops=4 * rows * width * rows * blocks + extra,
        bytes_accessed=2 * MIB,
        transcendentals=rows * (width // HEAD) * rows * blocks,
    )


def attend(q, sources, distances, prev=None, weight=None, last=False, limit=8):
    rows, width = q.shape
    heads = width // (4 * HEAD)
    wide = pl.BlockSpec((rows, 4 * HEAD), lambda g: (0, g))
    args, specs = [q], [wide]
    for s in sources:
        a, sp = kv_specs(s, rows)
        args += a
        specs += sp
    if prev is not None:
        args += list(prev)
        specs += [wide] * 3
    if last:
        outs, out_specs = [pltpu.VMEM((rows, width), BF16)], [wide]
        body = functools.partial(last_kernel, distances)
    else:
        outs, out_specs = [pltpu.VMEM((rows, width), F32)] * 3, [wide] * 3
        body = functools.partial(part_kernel, distances, prev is not None, weight is not None)
    scratch = []
    if weight is not None:
        args.append(pltpu.with_memory_space_constraint(weight, pltpu.HBM))
        specs.append(ANY)
        outs.append(pltpu.VMEM(weight.shape, weight.dtype))
        out_specs.append(WHOLE)
        scratch.append(pltpu.SemaphoreType.DMA(()))
    return pl.pallas_call(
        body,
        grid=(heads,),
        out_shape=tuple(outs),
        in_specs=specs,
        out_specs=tuple(out_specs),
        scratch_shapes=scratch,
        cost_estimate=cost(rows, width, len(sources)),
        compiler_params=pltpu.CompilerParams(vmem_limit_bytes=limit * MIB),
    )(*args)


def project_partner(att, weight, limit=8):
    rows, half = att.shape[0], weight.shape[1] // 2
    return pl.pallas_call(
        partner_kernel,
        out_shape=pltpu.VMEM((rows, half), BF16),
        in_specs=[WHOLE] * 2,
        out_specs=WHOLE,
        cost_estimate=pl.CostEstimate(
            flops=2 * rows * weight.shape[0] * half, bytes_accessed=2 * MIB, transcendentals=0
        ),
        compiler_params=pltpu.CompilerParams(vmem_limit_bytes=limit * MIB),
    )(att, weight)


def project_own(att, weight, residual, limit=8):
    rows, half = residual.shape
    return pl.pallas_call(
        own_kernel,
        out_shape=pltpu.VMEM((rows, half), F32),
        in_specs=[WHOLE] * 3,
        out_specs=WHOLE,
        cost_estimate=pl.CostEstimate(
            flops=2 * rows * weight.shape[0] * half, bytes_accessed=2 * MIB, transcendentals=0
        ),
        compiler_params=pltpu.CompilerParams(vmem_limit_bytes=limit * MIB),
    )(att, weight, residual)


def on_device(queries, keys, values, residual, out_weight):
  up = route("ctx", lambda i: i + 4)
  ring1 = route("ctx", lambda i: i // 4 * 4 + (i + 1) % 4)
  ring2 = route("ctx", lambda i: i // 4 * 4 + (i + 2) % 4)
  both = packed(keys, values)
  back4 = lax.ppermute(both, "ctx", up)
  key1 = lax.ppermute(keys, "ctx", route("ctx", lambda i: i + 1))
  *state, weight = attend(queries, [(keys, values)], (0,), weight=out_weight)
  back8 = lax.ppermute(back4, "ctx", up)
  two, one = chosen(both, back4)
  back2 = lax.ppermute(two, "ctx", ring2)
  value1 = lax.ppermute(one, "ctx", ring1)
  state = attend(queries, [back4], (4,), state)
  (attended,) = attend(queries, [(key1, value1), back2, back8], (1, 2, 8), state, last=True)
  sent = project_partner(attended, weight)
  received = lax.ppermute(sent, "hid", [(0, 1), (1, 0)])
  kept = project_own(attended, weight, residual)
  return (kept + received.astype(F32)).astype(BF16)


def solution(mesh):
    return jax.shard_map(
        on_device,
        mesh=mesh,
        in_specs=(P("ctx", "hid"), P("ctx", "hid"), P("ctx", "hid"), P("ctx", "hid"), P("hid", None)),
        out_specs=P("ctx", "hid"),
        check_vma=False,
    )
```

time: 113 us -> 65.8 us (0.58)
  the two profiles are of different devices: /device:TPU:391 before, /device:TPU:257 now
where the time goes in v1:
time: 65.8 us; the launch traced here: 65.5 us
  Pallas kernels  23.7 us (36%)
  waiting for transfers between devices  21.9 us (33%)
  starting transfers between devices  18.5 us (28%)
  other arithmetic  1.29 us (2%)
    pallas_call x3, Pallas kernels, attend(): pl.pallas_call(body, grid=(heads,), out_shape=tuple(outs), in_specs=specs...  16.7 us
    ppermute x1, waiting for transfers between devices, on_device(): back4 = lax.ppermute(both, 'ctx', up)  14.8 us
    ppermute x1, waiting for transfers between devices, on_device(): key1 = lax.ppermute(keys, 'ctx', route('ctx', lambda i: i + 1))  7.05 us
    ppermute x1, starting transfers between devices, on_device(): back2 = lax.ppermute(two, 'ctx', ring2)  4.65 us
    ppermute x1, starting transfers between devices, on_device(): received = lax.ppermute(sent, 'hid', [(0, 1), (1, 0)])  4.58 us
    ppermute x1, starting transfers between devices, on_device(): back4 = lax.ppermute(both, 'ctx', up)  3.2 us
    pallas_call x1, Pallas kernels, project_own(): pl.pallas_call(own_kernel, out_shape=pltpu.VMEM((rows, half), F32), in_sp...  2.87 us
    pallas_call x1, Pallas kernels, project_partner(): pl.pallas_call(partner_kernel, out_shape=pltpu.VMEM((rows, half), BF16),...  2.87 us
  transfers between devices with their start and end apart: 6, of which 2 were waited for; matrix products, arithmetic and copies ran while one was open for 0% of the time, Pallas kernels for 19%

profile of v1, /device:TPU:257, one launch (start us, length us, event | category | flops | bytes accessed | tf_op | source)
XLA Modules:
  0.0 65.5 jit_solution(17275587840929601246)
XLA Ops:
  0.0 0.0 copy-start.2
  0.0 0.0 copy-start.1
  0.0 0.0 copy-start
  0.0 1.2 %shard_map.55.both_ref = bf16[512,512]{1,0:T(8,128)(2,1)S(1)} custom-call(bf16[256,512]{1,0:T(8,128)(2,1)} %refs_1_.1, bf16[256,512]{1,0:T(8,128)(2,1)} %refs_2_.1), custom_call_target="tpu_custom_call" | custom-call | tf_op jit(solution)/shard_map/pallas_call | solution.py:199
  1.2 3.2 %collective-permute-start.1 = (bf16[512,512]{1,0:T(8,128)(2,1)S(1)}, bf16[512,512]{1,0:T(8,128)(2,1)S(1)}, u32[]{:S(2)}, u32[]{:S(2)}) collective-permute-start(bf16[512,512]{1,0:T(8,128)(2,1)S(1)} %shard_map.55.both_ref), channel_id=1, source_target_pairs={{0,8},{2,10},{4,12},{6,14},{8,16},{10,18},{12,20},{14,22},{16,24},... | collective-permute-start | bytes 1572872 | tf_op jit(solution)/shard_map/ppermute | solution.py:298
  4.4 14.8 %collective-permute-done.1.back_ref.refs_1_.refs_2_ = bf16[512,512]{1,0:T(8,128)(2,1)S(1)} collective-permute-done((bf16[512,512]{1,0:T(8,128)(2,1)S(1)}, bf16[512,512]{1,0:T(8,128)(2,1)S(1)}, u32[]{:S(2)}, u32[]{:S(2)}) %collective-permute-start.1) | collective-permute-done | bytes 524320 | tf_op jit(solution)/shard_map/ppermute | solution.py:298
  19.2 0.1 shard_map.56
  19.3 4.6 %collective-permute-start.3 = (bf16[512,512]{1,0:T(8,128)(2,1)S(1)}, bf16[512,512]{1,0:T(8,128)(2,1)S(1)}, u32[]{:S(2)}, u32[]{:S(2)}) collective-permute-start(bf16[512,512]{1,0:T(8,128)(2,1)S(1)} %get-tuple-element.15), channel_id=1, source_target_pairs={{0,4},{2,6},{4,0},{6,2},{8,12},{10,14},{12,8},{14,10},{16,20},{18,... | collective-permute-start | bytes 1572872 | tf_op jit(solution)/shard_map/ppermute | solution.py:303
  23.9 1.9 %collective-permute-start.4 = (bf16[512,512]{1,0:T(8,128)(2,1)S(1)}, bf16[512,512]{1,0:T(8,128)(2,1)S(1)}, u32[]{:S(2)}, u32[]{:S(2)}) collective-permute-start(bf16[512,512]{1,0:T(8,128)(2,1)S(1)} %collective-permute-done.1.back_ref.refs_1_.refs_2_), channel_id=1, source_target_pairs={{0,8},{2,10},{4,12},{6,14},{8,16},{10,18},{12,20},{14,22},{16,24},... | collective-permute-start | bytes 1572872 | tf_op jit(solution)/shard_map/ppermute | solution.py:301
  25.9 0.0 copy-done.2
  25.9 2.2 %collective-permute-start = (bf16[256,512]{1,0:T(8,128)(2,1)S(1)}, bf16[256,512]{1,0:T(8,128)(2,1)S(1)}, u32[]{:S(2)}, u32[]{:S(2)}) collective-permute-start(bf16[256,512]{1,0:T(8,128)(2,1)S(1)} %copy-done.2), channel_id=1, source_target_pairs={{0,2},{2,4},{4,6},{6,8},{8,10},{10,12},{12,14},{14,16},{16,18},{18... | collective-permute-start | bytes 786440 | tf_op jit(solution)/shard_map/ppermute | solution.py:299
  28.1 1.9 %collective-permute-start.2 = (bf16[256,512]{1,0:T(8,128)(2,1)S(1)}, bf16[256,512]{1,0:T(8,128)(2,1)S(1)}, u32[]{:S(2)}, u32[]{:S(2)}) collective-permute-start(bf16[256,512]{1,0:T(8,128)(2,1)S(1)} %get-tuple-element.14), channel_id=1, source_target_pairs={{0,2},{2,4},{4,6},{6,0},{8,10},{10,12},{12,14},{14,8},{16,18},{18,... | collective-permute-start | bytes 786440 | tf_op jit(solution)/shard_map/ppermute | solution.py:304
  30.0 0.0 copy-done.1
  30.0 0.0 copy-done
  30.0 6.0 %shard_map.57 = (f32[256,2048]{1,0:T(8,128)S(1)}, f32[256,2048]{1,0:T(8,128)S(1)}, f32[256,2048]{1,0:T(8,128)S(1)}, bf16[2048,4096]{1,0:T(8,128)(2,1)S(1)}) custom-call(bf16[256,2048]{1,0:T(8,128)(2,1)S(1)} %copy-done, bf16[256,512]{1,0:T(8,128)(2,1)S(1)} %copy-done.2, bf16[256,512]{1,0:T(8,128)(2,1)S(1)} %copy-done.1, bf16[2048,4096]{1,0:T(8,128)(2,1)} %refs_3_.1), custom_call_target="tpu_custom_call" | custom-call | flops 536870912 | bytes 2097152 | tf_op jit(solution)/shard_map/pallas_call | solution.py:253
  36.1 3.9 %shard_map.58 = (f32[256,2048]{1,0:T(8,128)S(1)}, f32[256,2048]{1,0:T(8,128)S(1)}, f32[256,2048]{1,0:T(8,128)S(1)}) custom-call(bf16[256,2048]{1,0:T(8,128)(2,1)S(1)} %copy-done, bf16[512,512]{1,0:T(8,128)(2,1)S(1)} %collective-permute-done.1.back_ref.refs_1_.refs_2_, bf16[512,512]{1,0:T(8,128)(2,1)S(1)} %collective-permute-done.1.back_ref.refs_1_.refs_2_, ...), custom_call_target="tpu_custom_call" | custom-call | flops 536870912 | bytes 2097152 | tf_op jit(solution)/shard_map/pallas_call | solution.py:253
  40.0 7.1 %collective-permute-done.refs_0_ = bf16[256,512]{1,0:T(8,128)(2,1)S(1)} collective-permute-done((bf16[256,512]{1,0:T(8,128)(2,1)S(1)}, bf16[256,512]{1,0:T(8,128)(2,1)S(1)}, u32[]{:S(2)}, u32[]{:S(2)}) %collective-permute-start) | collective-permute-done | bytes 262176 | tf_op jit(solution)/shard_map/ppermute | solution.py:299
  47.0 0.0 collective-permute-done.2.refs_1_
  47.0 0.0 collective-permute-done.3.refs_2_.refs_3_
  47.0 0.0 collective-permute-done.4.refs_4_.refs_5_
  47.0 6.8 %shard_map.59.att_ref = bf16[256,2048]{1,0:T(8,128)(2,1)S(1)} custom-call(bf16[256,2048]{1,0:T(8,128)(2,1)S(1)} %copy-done, bf16[256,512]{1,0:T(8,128)(2,1)S(1)} %collective-permute-done.refs_0_, bf16[256,512]{1,0:T(8,128)(2,1)S(1)} %collective-permute-done.2.refs_1_, bf16[512,512]{1,0:T(8,128)(2,1)S(1)} %collective-permute-done.3.refs_2_.refs_3_, ...), custom_call_target="tpu_custom_call" | custom-call | flops 1610612736 | bytes 2097152 | tf_op jit(solution)/shard_map/pallas_call | solution.py:253
  53.9 0.0 copy-start.3
  53.9 2.9 %shard_map.61 = bf16[256,2048]{1,0:T(8,128)(2,1)S(1)} custom-call(bf16[256,2048]{1,0:T(8,128)(2,1)S(1)} %shard_map.59.att_ref, bf16[2048,4096]{1,0:T(8,128)(2,1)S(1)} %get-tuple-element.22.w_ref), custom_call_target="tpu_custom_call" | custom-call | flops 2147483648 | bytes 2097152 | tf_op jit(solution)/shard_map/pallas_call | solution.py:267
  56.8 4.6 %collective-permute-start.5 = (bf16[256,2048]{1,0:T(8,128)(2,1)S(1)}, bf16[256,2048]{1,0:T(8,128)(2,1)S(1)}, u32[]{:S(2)}, u32[]{:S(2)}) collective-permute-start(bf16[256,2048]{1,0:T(8,128)(2,1)S(1)} %shard_map.61), channel_id=1, source_target_pairs={{0,1},{1,0},{2,3},{3,2},{4,5},{5,4},{6,7},{7,6},{8,9},{9,8},{10,11... | collective-permute-start | bytes 3145736 | tf_op jit(solution)/shard_map/ppermute | solution.py:308
  61.4 0.0 copy-done.3
  61.4 2.9 %shard_map.60 = f32[256,2048]{1,0:T(8,128)S(1)} custom-call(bf16[256,2048]{1,0:T(8,128)(2,1)S(1)} %shard_map.59.att_ref, bf16[2048,4096]{1,0:T(8,128)(2,1)S(1)} %get-tuple-element.22.w_ref, bf16[256,2048]{1,0:T(8,128)(2,1)S(1)} %copy-done.3), custom_call_target="tpu_custom_call" | custom-call | flops 2147483648 | bytes 2097152 | tf_op jit(solution)/shard_map/pallas_call | solution.py:281
  64.2 0.0 collective-permute-done.5
  64.2 1.3 %add_convert_fusion = bf16[256,2048]{1,0:T(8,128)(2,1)} fusion(f32[256,2048]{1,0:T(8,128)S(1)} %shard_map.60, bf16[256,2048]{1,0:T(8,128)(2,1)S(1)} %collective-permute-done.5), kind=kLoop, calls=%fused_computation | loop fusion | flops 1572864 | bytes 4194304 | tf_op jit(solution)/shard_map/convert_element_type | solution.py:310
Async XLA Ops:
  0.0 25.9 %copy-start.2 = (bf16[256,512]{1,0:T(8,128)(2,1)S(1)}, bf16[256,512]{1,0:T(8,128)(2,1)}, u32[]{:S(2)}) copy-start(bf16[256,512]{1,0:T(8,128)(2,1)} %refs_1_.1) | copy-start | bytes 786436
  0.0 30.0 %copy-start.1 = (bf16[256,512]{1,0:T(8,128)(2,1)S(1)}, bf16[256,512]{1,0:T(8,128)(2,1)}, u32[]{:S(2)}) copy-start(bf16[256,512]{1,0:T(8,128)(2,1)} %refs_2_.1) | copy-start | bytes 786436
  0.0 30.0 %copy-start = (bf16[256,2048]{1,0:T(8,128)(2,1)S(1)}, bf16[256,2048]{1,0:T(8,128)(2,1)}, u32[]{:S(2)}) copy-start(bf16[256,2048]{1,0:T(8,128)(2,1)} %q_ref.1) | copy-start | bytes 3145732
  1.2 18.0 %collective-permute-start.1 = (bf16[512,512]{1,0:T(8,128)(2,1)S(1)}, bf16[512,512]{1,0:T(8,128)(2,1)S(1)}, u32[]{:S(2)}, u32[]{:S(2)}) collective-permute-start(bf16[512,512]{1,0:T(8,128)(2,1)S(1)} %shard_map.55.both_ref), channel_id=1, source_target_pairs={{0,8},{2,10},{4,12},{6,14},{8,16},{10,18},{12,20},{14,22},{16,24},... | collective-permute-start | bytes 1572872 | tf_op jit(solution)/shard_map/ppermute | solution.py:298
  19.3 27.7 %collective-permute-start.3 = (bf16[512,512]{1,0:T(8,128)(2,1)S(1)}, bf16[512,512]{1,0:T(8,128)(2,1)S(1)}, u32[]{:S(2)}, u32[]{:S(2)}) collective-permute-start(bf16[512,512]{1,0:T(8,128)(2,1)S(1)} %get-tuple-element.15), channel_id=1, source_target_pairs={{0,4},{2,6},{4,0},{6,2},{8,12},{10,14},{12,8},{14,10},{16,20},{18,... | collective-permute-start | bytes 1572872 | tf_op jit(solution)/shard_map/ppermute | solution.py:303
  23.9 23.1 %collective-permute-start.4 = (bf16[512,512]{1,0:T(8,128)(2,1)S(1)}, bf16[512,512]{1,0:T(8,128)(2,1)S(1)}, u32[]{:S(2)}, u32[]{:S(2)}) collective-permute-start(bf16[512,512]{1,0:T(8,128)(2,1)S(1)} %collective-permute-done.1.back_ref.refs_1_.refs_2_), channel_id=1, source_target_pairs={{0,8},{2,10},{4,12},{6,14},{8,16},{10,18},{12,20},{14,22},{16,24},... | collective-permute-start | bytes 1572872 | tf_op jit(solution)/shard_map/ppermute | solution.py:301
  25.9 21.1 %collective-permute-start = (bf16[256,512]{1,0:T(8,128)(2,1)S(1)}, bf16[256,512]{1,0:T(8,128)(2,1)S(1)}, u32[]{:S(2)}, u32[]{:S(2)}) collective-permute-start(bf16[256,512]{1,0:T(8,128)(2,1)S(1)} %copy-done.2), channel_id=1, source_target_pairs={{0,2},{2,4},{4,6},{6,8},{8,10},{10,12},{12,14},{14,16},{16,18},{18... | collective-permute-start | bytes 786440 | tf_op jit(solution)/shard_map/ppermute | solution.py:299
  28.1 18.9 %collective-permute-start.2 = (bf16[256,512]{1,0:T(8,128)(2,1)S(1)}, bf16[256,512]{1,0:T(8,128)(2,1)S(1)}, u32[]{:S(2)}, u32[]{:S(2)}) collective-permute-start(bf16[256,512]{1,0:T(8,128)(2,1)S(1)} %get-tuple-element.14), channel_id=1, source_target_pairs={{0,2},{2,4},{4,6},{6,0},{8,10},{10,12},{12,14},{14,8},{16,18},{18,... | collective-permute-start | bytes 786440 | tf_op jit(solution)/shard_map/ppermute | solution.py:304
  53.9 7.5 %copy-start.3 = (bf16[256,2048]{1,0:T(8,128)(2,1)S(1)}, bf16[256,2048]{1,0:T(8,128)(2,1)}, u32[]{:S(2)}) copy-start(bf16[256,2048]{1,0:T(8,128)(2,1)} %res_ref.1) | copy-start | bytes 3145732
  56.8 7.5 %collective-permute-start.5 = (bf16[256,2048]{1,0:T(8,128)(2,1)S(1)}, bf16[256,2048]{1,0:T(8,128)(2,1)S(1)}, u32[]{:S(2)}, u32[]{:S(2)}) collective-permute-start(bf16[256,2048]{1,0:T(8,128)(2,1)S(1)} %shard_map.61), channel_id=1, source_target_pairs={{0,1},{1,0},{2,3},{3,2},{4,5},{5,4},{6,7},{7,6},{8,9},{9,8},{10,11... | collective-permute-start | bytes 3145736 | tf_op jit(solution)/shard_map/ppermute | solution.py:308

commit v2 on v0

v2 whole, which is shorter than its diff:
```python
import functools
import math

import jax
import jax.numpy as jnp
from jax import lax
from jax.experimental import pallas as pl
from jax.experimental.pallas import tpu as pltpu
from jax.sharding import PartitionSpec as P


HEAD = 128
GROUP = 4
SCALE = math.log2(math.e) / math.sqrt(HEAD)
MIB = 1 << 20
F32, BF16 = jnp.float32, jnp.bfloat16
WHOLE = pl.BlockSpec(memory_space=pltpu.VMEM)
IN_HBM = pl.BlockSpec(memory_space=pltpu.HBM)


def params(limit):
    return pltpu.CompilerParams(vmem_limit_bytes=limit * MIB)


def hbm(x):
    return pltpu.with_memory_space_constraint(x, pltpu.HBM)


def route(axis, target):
    n = lax.axis_size(axis)
    return [(i, target(i)) for i in range(n) if 0 <= target(i) < n]


def columns(start, size):
    return pl.ds(pl.multiple_of(start, HEAD), size)


def softmax_units(q_ref, g, blocks, prev):
    rows, tile = q_ref.shape[0], 128
    units = [(j, r) for j in range(GROUP) for r in range(0, rows, tile)]

    def scores_of(unit):
        j, r = unit
        at = (g * GROUP + j) * HEAD
        q = q_ref[r : r + tile, at : at + HEAD]
        out = []
        for key, _, own in blocks:
            n = r + tile if own else rows
            s = lax.dot_general(q, key[:n], (((1,), (1,)), ((), ())), preferred_element_type=F32)
            if own:
                row = lax.broadcasted_iota(jnp.int32, (tile, n), 0) + r
                s = jnp.where(lax.broadcasted_iota(jnp.int32, (tile, n), 1) <= row, s, -1e30)
            out.append(s)
        return jnp.concatenate(out, axis=1)

    ahead = scores_of(units[0])
    for i, (j, r) in enumerate(units):
        s = ahead
        where = (pl.ds(r, tile), pl.ds((g * GROUP + j) * HEAD, HEAD))
        top = functools.reduce(
            jnp.maximum, [s[:, t : t + HEAD] for t in range(0, s.shape[1], HEAD)]
        )
        m = jnp.broadcast_to(jnp.max(top, axis=1, keepdims=True), top.shape)
        if prev is not None:
            acc0, m0, l0 = (ref[where] for ref in prev)
            m = jnp.maximum(m, m0)
        mc = m * SCALE
        p = jnp.exp2(s * SCALE - jnp.concatenate([mc] * (s.shape[1] // HEAD), axis=1)).astype(BF16)
        values = jnp.concatenate([w[: r + tile if own else rows] for _, w, own in blocks], axis=0)
        total = jnp.dot(p, values, preferred_element_type=F32)
        acc, l = total[:, :HEAD], total[:, HEAD:]
        if prev is not None:
            alpha = jnp.exp2(m0 * SCALE - mc)
            acc = acc + alpha * acc0
            l = l + alpha * l0
        yield where, (acc, m, l)
        if i + 1 < len(units):
            ahead = scores_of(units[i + 1])


def head_blocks(g, pairs, distances, first_ref):
    at = pl.ds(g * HEAD, HEAD)
    rows = first_ref.shape[0]
    position = lax.axis_index("ctx")
    out = []
    for (k_ref, v_ref), d in zip(pairs, distances):
        k, v, ones = k_ref[:, at], v_ref[:, at], jnp.ones((rows, HEAD), BF16)
        if d:
            there = position >= d
            first = jnp.broadcast_to(first_ref[0:1, at], k.shape)
            k = jnp.where(there, k, first)
            v = jnp.where(there, v, jnp.zeros_like(v))
            ones = jnp.where(there, ones, jnp.zeros_like(ones))
        out.append((k, jnp.concatenate([v, ones], axis=1), d == 0))
    return out


def split_pairs(refs, stacked):
    pairs = []
    for both in stacked:
        if both:
            ref = refs.pop(0)
            rows = ref.shape[0] // 2
            pairs.append((ref.at[pl.ds(0, rows)], ref.at[pl.ds(rows, rows)]))
        else:
            pairs.append((refs.pop(0), refs.pop(0)))
    return pairs


def own_kernel(q_ref, k_ref, v_ref, w_hbm, acc_ref, m_ref, l_ref, w_ref, sem):
    copy = pltpu.make_async_copy(w_hbm, w_ref, sem)
    copy.start()
    for g in range(k_ref.shape[1] // HEAD):
        blocks = head_blocks(g, [(k_ref, v_ref)], (0,), k_ref)
        for where, new in softmax_units(q_ref, g, blocks, None):
            for ref, value in zip((acc_ref, m_ref, l_ref), new):
                ref[where] = value
    copy.wait()


def middle_kernel(distances, stacked, q_ref, first_ref, *refs):
    refs = list(refs)
    pairs = split_pairs(refs, stacked)
    prev, state = refs[:3], refs[3:]
    for g in range(first_ref.shape[1] // HEAD):
        blocks = head_blocks(g, pairs, distances, first_ref)
        for where, new in softmax_units(q_ref, g, blocks, prev):
            for ref, value in zip(state, new):
                ref[where] = value


def last_kernel(distances, stacked, q_ref, first_ref, *refs):
    refs = list(refs)
    pairs = split_pairs(refs, stacked)
    prev, (w_ref, att_ref, send_ref) = refs[:3], refs[3:]
    for g in range(first_ref.shape[1] // HEAD):
        blocks = head_blocks(g, pairs, distances, first_ref)
        for where, (acc, _, l) in softmax_units(q_ref, g, blocks, prev):
            att_ref[where] = (acc / l).astype(BF16)
    width = send_ref.shape[1]
    base = (1 - lax.axis_index("hid")) * width
    tile = 512

    @pl.loop(0, width // tile)
    def _(t):
        send_ref[:, columns(t * tile, tile)] = jnp.dot(
            att_ref[...], w_ref[:, columns(base + t * tile, tile)], preferred_element_type=F32
        ).astype(BF16)


def kept_kernel(att_ref, w_ref, res_ref, out_ref):
    width = out_ref.shape[1]
    base = lax.axis_index("hid") * width
    tile = 512

    @pl.loop(0, width // tile)
    def _(t):
        here = columns(t * tile, tile)
        out_ref[:, here] = res_ref[:, here].astype(F32) + jnp.dot(
            att_ref[...], w_ref[:, columns(base + t * tile, tile)], preferred_element_type=F32
        )


def stage_kernel(*refs):
    n = len(refs) // 2
    *refs, sems = refs
    copies = [pltpu.make_async_copy(refs[i], refs[n + i], sems.at[i]) for i in range(n)]
    for c in copies:
        c.start()
    for c in copies:
        c.wait()


def choose(limit, mine_ref, back_ref, out_ref):
    column = lax.rem(lax.axis_index("ctx"), 4)

    @pl.when(column < limit)
    def _():
        out_ref[...] = mine_ref[...]

    @pl.when(column >= limit)
    def _():
        out_ref[...] = back_ref[...]


def staged(*arrays):
    return pl.pallas_call(
        stage_kernel,
        out_shape=tuple(pltpu.VMEM(a.shape, a.dtype) for a in arrays),
        in_specs=[IN_HBM] * len(arrays),
        out_specs=(WHOLE,) * len(arrays),
        scratch_shapes=[pltpu.SemaphoreType.DMA((len(arrays),))],
        compiler_params=params(2),
    )(*map(hbm, arrays))


def chosen_keys(mine, back):
    def kernel(mine_ref, back_ref, out_ref):
        choose(2, mine_ref, back_ref, out_ref)

    return pl.pallas_call(
        kernel,
        out_shape=pltpu.VMEM(mine.shape, mine.dtype),
        in_specs=[WHOLE] * 2,
        out_specs=WHOLE,
        compiler_params=params(2),
    )(mine, back)


def chosen_values(mine, back_keys, back):
    rows, width = mine.shape

    def kernel(mine_ref, back_keys_ref, back_ref, two_ref, one_ref, both_ref):
        choose(2, mine_ref, back_ref, two_ref)
        choose(3, mine_ref, back_ref, one_ref)
        both_ref[0:rows] = back_keys_ref[...]
        both_ref[rows:] = back_ref[...]

    one = pltpu.VMEM(mine.shape, mine.dtype)
    return pl.pallas_call(
        kernel,
        out_shape=(one, one, pltpu.VMEM((2 * rows, width), mine.dtype)),
        in_specs=[WHOLE] * 3,
        out_specs=(WHOLE,) * 3,
        compiler_params=params(2),
    )(mine, back_keys, back)


def estimate(rows, width, blocks, more=0):
    return pl.CostEstimate(
        flops=4 * rows * width * rows * blocks + more,
        bytes_accessed=2 * MIB,
        transcendentals=rows * (width // HEAD) * rows * blocks,
    )


def state_of(q):
    return [pltpu.VMEM(q.shape, F32)] * 3


def attend_own(q, keys, values, weight):
    return pl.pallas_call(
        own_kernel,
        out_shape=(*state_of(q), pltpu.VMEM(weight.shape, weight.dtype)),
        in_specs=[WHOLE] * 3 + [IN_HBM],
        out_specs=(WHOLE,) * 4,
        scratch_shapes=[pltpu.SemaphoreType.DMA(())],
        cost_estimate=estimate(*q.shape, 1),
        compiler_params=params(8),
    )(q, keys, values, hbm(weight))


def flat(sources):
    stacked = tuple(not isinstance(s, tuple) for s in sources)
    return stacked, [a for s in sources for a in (s if isinstance(s, tuple) else (s,))]


def attend_middle(q, first, sources, distances, state):
    stacked, arrays = flat(sources)
    return pl.pallas_call(
        functools.partial(middle_kernel, distances, stacked),
        out_shape=tuple(state_of(q)),
        in_specs=[WHOLE] * (5 + len(arrays)),
        out_specs=(WHOLE,) * 3,
        cost_estimate=estimate(*q.shape, len(sources)),
        compiler_params=params(8),
    )(q, first, *arrays, *state)


def attend_last(q, first, sources, distances, state, weight):
    stacked, arrays = flat(sources)
    rows, width = q.shape
    half = weight.shape[1] // 2
    return pl.pallas_call(
        functools.partial(last_kernel, distances, stacked),
        out_shape=(pltpu.VMEM(q.shape, BF16), pltpu.VMEM((rows, half), BF16)),
        in_specs=[WHOLE] * (6 + len(arrays)),
        out_specs=(WHOLE,) * 2,
        cost_estimate=estimate(rows, width, len(sources), 2 * rows * width * half),
        compiler_params=params(8),
    )(q, first, *arrays, *state, weight)


def project_kept(att, weight, residual):
    rows, half = residual.shape
    return pl.pallas_call(
        kept_kernel,
        out_shape=pltpu.VMEM((rows, half), F32),
        in_specs=[WHOLE] * 3,
        out_specs=WHOLE,
        cost_estimate=pl.CostEstimate(
            flops=2 * rows * weight.shape[0] * half, bytes_accessed=2 * MIB, transcendentals=0
        ),
        compiler_params=params(4),
    )(att, weight, residual)


def on_device(queries, keys, values, residual, out_weight):
    up = route("ctx", lambda i: i + 4)
    ring1 = route("ctx", lambda i: i // 4 * 4 + (i + 1) % 4)
    ring2 = route("ctx", lambda i: i // 4 * 4 + (i + 2) % 4)
    keys4 = lax.ppermute(keys, "ctx", up)
    values4 = lax.ppermute(values, "ctx", up)
    keys1 = lax.ppermute(keys, "ctx", route("ctx", lambda i: i + 1))
    q, k, v = staged(queries, keys, values)
    two = chosen_keys(k, keys4)
    keys2 = lax.ppermute(two, "ctx", ring2)
    two, one, both = chosen_values(v, keys4, values4)
    values2 = lax.ppermute(two, "ctx", ring2)
    back8 = lax.ppermute(both, "ctx", up)
    values1 = lax.ppermute(one, "ctx", ring1)
    *state, weight = attend_own(q, k, v, out_weight)
    state = attend_middle(q, k, [(keys4, values4)], (4,), state)
    attended, sent = attend_last(
        q, k, [(keys1, values1), (keys2, values2), back8], (1, 2, 8), state, weight
    )
    received = lax.ppermute(sent, "hid", [(0, 1), (1, 0)])
    kept = project_kept(attended, weight, residual)
    return (kept + received.astype(F32)).astype(BF16)


def solution(mesh):
    return jax.shard_map(
        on_device,
        mesh=mesh,
        in_specs=(P("ctx", "hid"), P("ctx", "hid"), P("ctx", "hid"), P("ctx", "hid"), P("hid", None)),
        out_specs=P("ctx", "hid"),
        check_vma=False,
    )
```

time: 113 us -> 68.5 us (0.61)
  the two profiles are of different devices: /device:TPU:391 before, /device:TPU:249 now
where the time goes in v2:
time: 68.5 us; the launch traced here: 68.1 us
  starting transfers between devices  31.7 us (46%)
  Pallas kernels  19.5 us (28%)
  waiting for transfers between devices  15.5 us (23%)
  other arithmetic  1.29 us (2%)
    ppermute x1, waiting for transfers between devices, on_device(): values1 = lax.ppermute(one, 'ctx', ring1)  9.2 us
    pallas_call x1, Pallas kernels, attend_last(): pl.pallas_call(functools.partial(last_kernel, distances, stacked), out_sh...  7.4 us
    ppermute x1, starting transfers between devices, on_device(): back8 = lax.ppermute(both, 'ctx', up)  7.32 us
    pallas_call x1, Pallas kernels, attend_own(): pl.pallas_call(own_kernel, out_shape=(*state_of(q), pltpu.VMEM(weight.sha...  5.78 us
    ppermute x1, waiting for transfers between devices, on_device(): values4 = lax.ppermute(values, 'ctx', up)  5.62 us
    ppermute x1, starting transfers between devices, on_device(): keys4 = lax.ppermute(keys, 'ctx', up)  4.53 us
    ppermute x1, starting transfers between devices, on_device(): keys2 = lax.ppermute(two, 'ctx', ring2)  3.63 us
    ppermute x1, starting transfers between devices, on_device(): received = lax.ppermute(sent, 'hid', [(0, 1), (1, 0)])  3.58 us
  transfers between devices with their start and end apart: 8, of which 3 were waited for; matrix products, arithmetic and copies ran while one was open for 0% of the time, Pallas kernels for 18%

profile of v2, /device:TPU:249, one launch (start us, length us, event | category | flops | bytes accessed | tf_op | source)
XLA Modules:
  0.0 68.1 jit_solution(13964875761912953657)
XLA Ops:
  0.0 0.0 copy-start.1
  0.0 4.5 %collective-permute-start.1 = (bf16[256,512]{1,0:T(8,128)(2,1)}, bf16[256,512]{1,0:T(8,128)(2,1)S(1)}, u32[]{:S(2)}, u32[]{:S(2)}) collective-permute-start(bf16[256,512]{1,0:T(8,128)(2,1)} %refs_1_.1), channel_id=1, source_target_pairs={{0,8},{2,10},{4,12},{6,14},{8,16},{10,18},{12,20},{14,22},{16,24},... | collective-permute-start | bytes 786440 | tf_op jit(solution)/shard_map/ppermute | solution.py:302
  4.5 3.2 %collective-permute-start.2 = (bf16[256,512]{1,0:T(8,128)(2,1)}, bf16[256,512]{1,0:T(8,128)(2,1)S(1)}, u32[]{:S(2)}, u32[]{:S(2)}) collective-permute-start(bf16[256,512]{1,0:T(8,128)(2,1)} %refs_2_.1), channel_id=1, source_target_pairs={{0,8},{2,10},{4,12},{6,14},{8,16},{10,18},{12,20},{14,22},{16,24},... | collective-permute-start | bytes 786440 | tf_op jit(solution)/shard_map/ppermute | solution.py:303
  7.8 1.4 %shard_map.55 = (bf16[256,2048]{1,0:T(8,128)(2,1)S(1)}, bf16[256,512]{1,0:T(8,128)(2,1)S(1)}, bf16[256,512]{1,0:T(8,128)(2,1)S(1)}) custom-call(bf16[256,2048]{1,0:T(8,128)(2,1)} %refs_0_.1, bf16[256,512]{1,0:T(8,128)(2,1)} %refs_1_.1, bf16[256,512]{1,0:T(8,128)(2,1)} %refs_2_.1), custom_call_target="tpu_custom_call" | custom-call | tf_op jit(solution)/shard_map/pallas_call | solution.py:187
  9.1 0.7 %collective-permute-done.1.back_keys_ref.back_ref.refs_0_ = bf16[256,512]{1,0:T(8,128)(2,1)S(1)} collective-permute-done((bf16[256,512]{1,0:T(8,128)(2,1)}, bf16[256,512]{1,0:T(8,128)(2,1)S(1)}, u32[]{:S(2)}, u32[]{:S(2)}) %collective-permute-start.1) | collective-permute-done | bytes 262176 | tf_op jit(solution)/shard_map/ppermute | solution.py:302
  9.8 5.6 %collective-permute-done.2.back_ref.refs_1_ = bf16[256,512]{1,0:T(8,128)(2,1)S(1)} collective-permute-done((bf16[256,512]{1,0:T(8,128)(2,1)}, bf16[256,512]{1,0:T(8,128)(2,1)S(1)}, u32[]{:S(2)}, u32[]{:S(2)}) %collective-permute-start.2) | collective-permute-done | bytes 262176 | tf_op jit(solution)/shard_map/ppermute | solution.py:303
  15.4 0.1 shard_map.56
  15.5 7.3 %collective-permute-start.6 = (bf16[512,512]{1,0:T(8,128)(2,1)S(1)}, bf16[512,512]{1,0:T(8,128)(2,1)S(1)}, u32[]{:S(2)}, u32[]{:S(2)}) collective-permute-start(bf16[512,512]{1,0:T(8,128)(2,1)S(1)} %get-tuple-element.25), channel_id=1, source_target_pairs={{0,8},{2,10},{4,12},{6,14},{8,16},{10,18},{12,20},{14,22},{16,24},... | collective-permute-start | bytes 1572872 | tf_op jit(solution)/shard_map/ppermute | solution.py:310
  22.9 0.0 copy-done.1
  22.9 3.1 %collective-permute-start = (bf16[256,512]{1,0:T(8,128)(2,1)S(1)}, bf16[256,512]{1,0:T(8,128)(2,1)S(1)}, u32[]{:S(2)}, u32[]{:S(2)}) collective-permute-start(bf16[256,512]{1,0:T(8,128)(2,1)S(1)} %copy-done.1), channel_id=1, source_target_pairs={{0,2},{2,4},{4,6},{6,8},{8,10},{10,12},{12,14},{14,16},{16,18},{18... | collective-permute-start | bytes 786440 | tf_op jit(solution)/shard_map/ppermute | solution.py:304
  26.0 3.1 %collective-permute-start.3 = (bf16[256,512]{1,0:T(8,128)(2,1)S(1)}, bf16[256,512]{1,0:T(8,128)(2,1)S(1)}, u32[]{:S(2)}, u32[]{:S(2)}) collective-permute-start(bf16[256,512]{1,0:T(8,128)(2,1)S(1)} %get-tuple-element.23), channel_id=1, source_target_pairs={{0,2},{2,4},{4,6},{6,0},{8,10},{10,12},{12,14},{14,8},{16,18},{18,... | collective-permute-start | bytes 786440 | tf_op jit(solution)/shard_map/ppermute | solution.py:311
  29.1 3.2 %collective-permute-start.5 = (bf16[256,512]{1,0:T(8,128)(2,1)S(1)}, bf16[256,512]{1,0:T(8,128)(2,1)S(1)}, u32[]{:S(2)}, u32[]{:S(2)}) collective-permute-start(bf16[256,512]{1,0:T(8,128)(2,1)S(1)} %get-tuple-element.24), channel_id=1, source_target_pairs={{0,4},{2,6},{4,0},{6,2},{8,12},{10,14},{12,8},{14,10},{16,20},{18,... | collective-permute-start | bytes 786440 | tf_op jit(solution)/shard_map/ppermute | solution.py:309
  32.3 3.6 %collective-permute-start.4 = (bf16[256,512]{1,0:T(8,128)(2,1)S(1)}, bf16[256,512]{1,0:T(8,128)(2,1)S(1)}, u32[]{:S(2)}, u32[]{:S(2)}) collective-permute-start(bf16[256,512]{1,0:T(8,128)(2,1)S(1)} %shard_map.57), channel_id=1, source_target_pairs={{0,4},{2,6},{4,0},{6,2},{8,12},{10,14},{12,8},{14,10},{16,20},{18,... | collective-permute-start | bytes 786440 | tf_op jit(solution)/shard_map/ppermute | solution.py:307
  36.0 5.8 %shard_map.58 = (f32[256,2048]{1,0:T(8,128)S(1)}, f32[256,2048]{1,0:T(8,128)S(1)}, f32[256,2048]{1,0:T(8,128)S(1)}, bf16[2048,4096]{1,0:T(8,128)(2,1)S(1)}) custom-call(bf16[256,2048]{1,0:T(8,128)(2,1)S(1)} %get-tuple-element.20.q_ref, bf16[256,512]{1,0:T(8,128)(2,1)S(1)} %get-tuple-element.21.mine_ref.k_ref.first_ref, ...), custom_call_target="tpu_custom_call" | custom-call | flops 536870912 | bytes 2097152 | tf_op jit(solution)/shard_map/pallas_call | solution.py:242
  41.8 1.9 %shard_map.59 = (f32[256,2048]{1,0:T(8,128)S(1)}, f32[256,2048]{1,0:T(8,128)S(1)}, f32[256,2048]{1,0:T(8,128)S(1)}) custom-call(bf16[256,2048]{1,0:T(8,128)(2,1)S(1)} %get-tuple-element.20.q_ref, bf16[256,512]{1,0:T(8,128)(2,1)S(1)} %get-tuple-element.21.mine_ref.k_ref.first_ref, bf16[256,512]{1,0:T(8,128)(2,1)S(1)} %collective-permute-done.1.back_keys_ref.back_ref.refs_0_, ...), custom_call_target="tpu_custom_call" | custom-call | flops 536870912 | bytes 2097152 | tf_op jit(solution)/shard_map/pallas_call | solution.py:260
  43.7 0.0 collective-permute-done.refs_0_
  43.7 9.2 %collective-permute-done.3.refs_1_ = bf16[256,512]{1,0:T(8,128)(2,1)S(1)} collective-permute-done((bf16[256,512]{1,0:T(8,128)(2,1)S(1)}, bf16[256,512]{1,0:T(8,128)(2,1)S(1)}, u32[]{:S(2)}, u32[]{:S(2)}) %collective-permute-start.3) | collective-permute-done | bytes 262176 | tf_op jit(solution)/shard_map/ppermute | solution.py:311
  52.9 0.0 collective-permute-done.5.refs_3_
  52.9 0.0 collective-permute-done.4.refs_2_
  52.9 0.0 collective-permute-done.6.refs_4_
  52.9 0.0 copy-start
  52.9 7.4 %shard_map.60 = (bf16[256,2048]{1,0:T(8,128)(2,1)S(1)}, bf16[256,2048]{1,0:T(8,128)(2,1)S(1)}) custom-call(bf16[256,2048]{1,0:T(8,128)(2,1)S(1)} %get-tuple-element.20.q_ref, bf16[256,512]{1,0:T(8,128)(2,1)S(1)} %get-tuple-element.21.mine_ref.k_ref.first_ref, bf16[256,512]{1,0:T(8,128)(2,1)S(1)} %collective-permute-done.refs_0_, ...), custom_call_target="tpu_custom_call" | custom-call | flops 3758096384 | bytes 2097152 | tf_op jit(solution)/shard_map/pallas_call | solution.py:274
  60.3 3.6 %collective-permute-start.7 = (bf16[256,2048]{1,0:T(8,128)(2,1)S(1)}, bf16[256,2048]{1,0:T(8,128)(2,1)S(1)}, u32[]{:S(2)}, u32[]{:S(2)}) collective-permute-start(bf16[256,2048]{1,0:T(8,128)(2,1)S(1)} %get-tuple-element.34), channel_id=1, source_target_pairs={{0,1},{1,0},{2,3},{3,2},{4,5},{5,4},{6,7},{7,6},{8,9},{9,8},{10,11... | collective-permute-start | bytes 3145736 | tf_op jit(solution)/shard_map/ppermute | solution.py:317
  63.9 0.0 copy-done
  63.9 2.9 %shard_map.61 = f32[256,2048]{1,0:T(8,128)S(1)} custom-call(bf16[256,2048]{1,0:T(8,128)(2,1)S(1)} %get-tuple-element.33.att_ref, bf16[2048,4096]{1,0:T(8,128)(2,1)S(1)} %get-tuple-element.32.refs_8_.w_ref, bf16[256,2048]{1,0:T(8,128)(2,1)S(1)} %copy-done), custom_call_target="tpu_custom_call" | custom-call | flops 2147483648 | bytes 2097152 | tf_op jit(solution)/shard_map/pallas_call | solution.py:286
  66.8 0.0 collective-permute-done.7
  66.8 1.3 %add_convert_fusion = bf16[256,2048]{1,0:T(8,128)(2,1)} fusion(f32[256,2048]{1,0:T(8,128)S(1)} %shard_map.61, bf16[256,2048]{1,0:T(8,128)(2,1)S(1)} %collective-permute-done.7), kind=kLoop, calls=%fused_computation | loop fusion | flops 1572864 | bytes 4194304 | tf_op jit(solution)/shard_map/convert_element_type | solution.py:319
  (1 shorter events, 0.0 us)
Async XLA Ops:
  0.0 22.9 %copy-start.1 = (bf16[256,512]{1,0:T(8,128)(2,1)S(1)}, bf16[256,512]{1,0:T(8,128)(2,1)}, u32[]{:S(2)}) copy-start(bf16[256,512]{1,0:T(8,128)(2,1)} %refs_1_.1) | copy-start | bytes 786436
  0.0 9.8 %collective-permute-start.1 = (bf16[256,512]{1,0:T(8,128)(2,1)}, bf16[256,512]{1,0:T(8,128)(2,1)S(1)}, u32[]{:S(2)}, u32[]{:S(2)}) collective-permute-start(bf16[256,512]{1,0:T(8,128)(2,1)} %refs_1_.1), channel_id=1, source_target_pairs={{0,8},{2,10},{4,12},{6,14},{8,16},{10,18},{12,20},{14,22},{16,24},... | collective-permute-start | bytes 786440 | tf_op jit(solution)/shard_map/ppermute | solution.py:302
  4.5 10.9 %collective-permute-start.2 = (bf16[256,512]{1,0:T(8,128)(2,1)}, bf16[256,512]{1,0:T(8,128)(2,1)S(1)}, u32[]{:S(2)}, u32[]{:S(2)}) collective-permute-start(bf16[256,512]{1,0:T(8,128)(2,1)} %refs_2_.1), channel_id=1, source_target_pairs={{0,8},{2,10},{4,12},{6,14},{8,16},{10,18},{12,20},{14,22},{16,24},... | collective-permute-start | bytes 786440 | tf_op jit(solution)/shard_map/ppermute | solution.py:303
  15.5 37.4 %collective-permute-start.6 = (bf16[512,512]{1,0:T(8,128)(2,1)S(1)}, bf16[512,512]{1,0:T(8,128)(2,1)S(1)}, u32[]{:S(2)}, u32[]{:S(2)}) collective-permute-start(bf16[512,512]{1,0:T(8,128)(2,1)S(1)} %get-tuple-element.25), channel_id=1, source_target_pairs={{0,8},{2,10},{4,12},{6,14},{8,16},{10,18},{12,20},{14,22},{16,24},... | collective-permute-start | bytes 1572872 | tf_op jit(solution)/shard_map/ppermute | solution.py:310
  22.9 20.8 %collective-permute-start = (bf16[256,512]{1,0:T(8,128)(2,1)S(1)}, bf16[256,512]{1,0:T(8,128)(2,1)S(1)}, u32[]{:S(2)}, u32[]{:S(2)}) collective-permute-start(bf16[256,512]{1,0:T(8,128)(2,1)S(1)} %copy-done.1), channel_id=1, source_target_pairs={{0,2},{2,4},{4,6},{6,8},{8,10},{10,12},{12,14},{14,16},{16,18},{18... | collective-permute-start | bytes 786440 | tf_op jit(solution)/shard_map/ppermute | solution.py:304
  26.0 26.9 %collective-permute-start.3 = (bf16[256,512]{1,0:T(8,128)(2,1)S(1)}, bf16[256,512]{1,0:T(8,128)(2,1)S(1)}, u32[]{:S(2)}, u32[]{:S(2)}) collective-permute-start(bf16[256,512]{1,0:T(8,128)(2,1)S(1)} %get-tuple-element.23), channel_id=1, source_target_pairs={{0,2},{2,4},{4,6},{6,0},{8,10},{10,12},{12,14},{14,8},{16,18},{18,... | collective-permute-start | bytes 786440 | tf_op jit(solution)/shard_map/ppermute | solution.py:311
  29.1 23.8 %collective-permute-start.5 = (bf16[256,512]{1,0:T(8,128)(2,1)S(1)}, bf16[256,512]{1,0:T(8,128)(2,1)S(1)}, u32[]{:S(2)}, u32[]{:S(2)}) collective-permute-start(bf16[256,512]{1,0:T(8,128)(2,1)S(1)} %get-tuple-element.24), channel_id=1, source_target_pairs={{0,4},{2,6},{4,0},{6,2},{8,12},{10,14},{12,8},{14,10},{16,20},{18,... | collective-permute-start | bytes 786440 | tf_op jit(solution)/shard_map/ppermute | solution.py:309
  32.3 20.6 %collective-permute-start.4 = (bf16[256,512]{1,0:T(8,128)(2,1)S(1)}, bf16[256,512]{1,0:T(8,128)(2,1)S(1)}, u32[]{:S(2)}, u32[]{:S(2)}) collective-permute-start(bf16[256,512]{1,0:T(8,128)(2,1)S(1)} %shard_map.57), channel_id=1, source_target_pairs={{0,4},{2,6},{4,0},{6,2},{8,12},{10,14},{12,8},{14,10},{16,20},{18,... | collective-permute-start | bytes 786440 | tf_op jit(solution)/shard_map/ppermute | solution.py:307
  52.9 11.0 %copy-start = (bf16[256,2048]{1,0:T(8,128)(2,1)S(1)}, bf16[256,2048]{1,0:T(8,128)(2,1)}, u32[]{:S(2)}) copy-start(bf16[256,2048]{1,0:T(8,128)(2,1)} %res_ref.1) | copy-start | bytes 3145732
  60.3 6.5 %collective-permute-start.7 = (bf16[256,2048]{1,0:T(8,128)(2,1)S(1)}, bf16[256,2048]{1,0:T(8,128)(2,1)S(1)}, u32[]{:S(2)}, u32[]{:S(2)}) collective-permute-start(bf16[256,2048]{1,0:T(8,128)(2,1)S(1)} %get-tuple-element.34), channel_id=1, source_target_pairs={{0,1},{1,0},{2,3},{3,2},{4,5},{5,4},{6,7},{7,6},{8,9},{9,8},{10,11... | collective-permute-start | bytes 3145736 | tf_op jit(solution)/shard_map/ppermute | solution.py:317

commit v3 on v2

--- a/solution.py
+++ b/solution.py
@@ -107,58 +107,75 @@
     return pairs
 
 
-def own_kernel(q_ref, k_ref, v_ref, w_hbm, acc_ref, m_ref, l_ref, w_ref, sem):
-    copy = pltpu.make_async_copy(w_hbm, w_ref, sem)
-    copy.start()
-    for g in range(k_ref.shape[1] // HEAD):
-        blocks = head_blocks(g, [(k_ref, v_ref)], (0,), k_ref)
-        for where, new in softmax_units(q_ref, g, blocks, None):
-            for ref, value in zip((acc_ref, m_ref, l_ref), new):
-                ref[where] = value
-    copy.wait()
-
-
-def middle_kernel(distances, stacked, q_ref, first_ref, *refs):
+def part_kernel(distances, has_prev, half, q_ref, first_ref, *refs):
     refs = list(refs)
-    pairs = split_pairs(refs, stacked)
-    prev, state = refs[:3], refs[3:]
+    pairs = [(refs.pop(0), refs.pop(0)) for _ in distances]
+    prev = [refs.pop(0) for _ in range(3)] if has_prev else None
+    w_hbm, *state, w_ref, sems = refs
+    size = w_ref.shape[0] // sems.shape[0]
+    copies = []
+    for i in range(sems.shape[0]):
+        source = w_hbm.at[pl.ds(half * w_ref.shape[0] + i * size, size)]
+        copies.append(pltpu.make_async_copy(source, w_ref.at[pl.ds(i * size, size)], sems.at[i]))
+        copies[-1].start()
     for g in range(first_ref.shape[1] // HEAD):
         blocks = head_blocks(g, pairs, distances, first_ref)
         for where, new in softmax_units(q_ref, g, blocks, prev):
             for ref, value in zip(state, new):
                 ref[where] = value
+    for c in copies:
+        c.wait()
+
+
+def product(att_ref, weights, at):
+    depth = weights[0].shape[0]
+    return sum(
+        jnp.dot(att_ref[:, i * depth : (i + 1) * depth], w[:, at], preferred_element_type=F32)
+        for i, w in enumerate(weights)
+    )
 
 
 def last_kernel(distances, stacked, q_ref, first_ref, *refs):
     refs = list(refs)
     pairs = split_pairs(refs, stacked)
-    prev, (w_ref, att_ref, send_ref) = refs[:3], refs[3:]
+    prev, (*weights, att_ref, send_ref) = refs[:3], refs[3:]
     for g in range(first_ref.shape[1] // HEAD):
         blocks = head_blocks(g, pairs, distances, first_ref)
         for where, (acc, _, l) in softmax_units(q_ref, g, blocks, prev):
             att_ref[where] = (acc / l).astype(BF16)
-    width = send_ref.shape[1]
+    width, tile = send_ref.shape[1], 512
     base = (1 - lax.axis_index("hid")) * width
-    tile = 512
 
     @pl.loop(0, width // tile)
     def _(t):
-        send_ref[:, columns(t * tile, tile)] = jnp.dot(
-            att_ref[...], w_ref[:, columns(base + t * tile, tile)], preferred_element_type=F32
+        send_ref[:, columns(t * tile, tile)] = product(
+            att_ref, weights, columns(base + t * tile, tile)
         ).astype(BF16)
 
 
-def kept_kernel(att_ref, w_ref, res_ref, out_ref):
-    width = out_ref.shape[1]
+def kept_kernel(att_ref, low_ref, high_ref, res_ref, out_ref):
+    width, tile = out_ref.shape[1], 512
     base = lax.axis_index("hid") * width
-    tile = 512
 
     @pl.loop(0, width // tile)
     def _(t):
         here = columns(t * tile, tile)
-        out_ref[:, here] = res_ref[:, here].astype(F32) + jnp.dot(
-            att_ref[...], w_ref[:, columns(base + t * tile, tile)], preferred_element_type=F32
+        out_ref[:, here] = res_ref[:, here].astype(F32) + product(
+            att_ref, (low_ref, high_ref), columns(base + t * tile, tile)
         )
+
+
+def add_kernel(kept_ref, got_ref, out_hbm, buf_ref, sems):
+    parts = sems.shape[0]
+    size = buf_ref.shape[0] // parts
+    copies = []
+    for i in range(parts):
+        at = pl.ds(i * size, size)
+        buf_ref[at] = (kept_ref[at] + got_ref[at].astype(F32)).astype(BF16)
+        copies.append(pltpu.make_async_copy(buf_ref.at[at], out_hbm.at[at], sems.at[i]))
+        copies[-1].start()
+    for c in copies:
+        c.wait()
 
 
 def stage_kernel(*refs):
@@ -238,16 +255,18 @@
     return [pltpu.VMEM(q.shape, F32)] * 3
 
 
-def attend_own(q, keys, values, weight):
-    return pl.pallas_call(
-        own_kernel,
-        out_shape=(*state_of(q), pltpu.VMEM(weight.shape, weight.dtype)),
-        in_specs=[WHOLE] * 3 + [IN_HBM],
+def attend_part(q, first, pairs, distances, state, weight, half):
+    arrays = [a for pair in pairs for a in pair]
+    rows = pltpu.VMEM((weight.shape[0] // 2, weight.shape[1]), weight.dtype)
+    return pl.pallas_call(
+        functools.partial(part_kernel, distances, bool(state), half),
+        out_shape=(*state_of(q), rows),
+        in_specs=[WHOLE] * (2 + len(arrays) + len(state)) + [IN_HBM],
         out_specs=(WHOLE,) * 4,
-        scratch_shapes=[pltpu.SemaphoreType.DMA(())],
-        cost_estimate=estimate(*q.shape, 1),
+        scratch_shapes=[pltpu.SemaphoreType.DMA((1,))],
+        cost_estimate=estimate(*q.shape, len(pairs)),
         compiler_params=params(8),
-    )(q, keys, values, hbm(weight))
+    )(q, first, *arrays, *state, hbm(weight))
 
 
 def flat(sources):
@@ -255,44 +274,46 @@
     return stacked, [a for s in sources for a in (s if isinstance(s, tuple) else (s,))]
 
 
-def attend_middle(q, first, sources, distances, state):
-    stacked, arrays = flat(sources)
-    return pl.pallas_call(
-        functools.partial(middle_kernel, distances, stacked),
-        out_shape=tuple(state_of(q)),
-        in_specs=[WHOLE] * (5 + len(arrays)),
-        out_specs=(WHOLE,) * 3,
-        cost_estimate=estimate(*q.shape, len(sources)),
-        compiler_params=params(8),
-    )(q, first, *arrays, *state)
-
-
-def attend_last(q, first, sources, distances, state, weight):
+def attend_last(q, first, sources, distances, state, weights):
     stacked, arrays = flat(sources)
     rows, width = q.shape
-    half = weight.shape[1] // 2
+    half = weights[0].shape[1] // 2
     return pl.pallas_call(
         functools.partial(last_kernel, distances, stacked),
         out_shape=(pltpu.VMEM(q.shape, BF16), pltpu.VMEM((rows, half), BF16)),
-        in_specs=[WHOLE] * (6 + len(arrays)),
+        in_specs=[WHOLE] * (7 + len(arrays)),
         out_specs=(WHOLE,) * 2,
         cost_estimate=estimate(rows, width, len(sources), 2 * rows * width * half),
         compiler_params=params(8),
-    )(q, first, *arrays, *state, weight)
-
-
-def project_kept(att, weight, residual):
+    )(q, first, *arrays, *state, *weights)
+
+
+def project_kept(att, weights, residual):
     rows, half = residual.shape
     return pl.pallas_call(
         kept_kernel,
         out_shape=pltpu.VMEM((rows, half), F32),
-        in_specs=[WHOLE] * 3,
+        in_specs=[WHOLE] * 4,
         out_specs=WHOLE,
         cost_estimate=pl.CostEstimate(
-            flops=2 * rows * weight.shape[0] * half, bytes_accessed=2 * MIB, transcendentals=0
+            flops=2 * rows * att.shape[1] * half, bytes_accessed=2 * MIB, transcendentals=0
         ),
         compiler_params=params(4),
-    )(att, weight, residual)
+    )(att, *weights, residual)
+
+
+def added(kept, received):
+    return pl.pallas_call(
+        add_kernel,
+        out_shape=jax.ShapeDtypeStruct(received.shape, received.dtype),
+        in_specs=[WHOLE] * 2,
+        out_specs=IN_HBM,
+        scratch_shapes=[
+            pltpu.VMEM(received.shape, received.dtype),
+            pltpu.SemaphoreType.DMA((4,)),
+        ],
+        compiler_params=params(4),
+    )(kept, received)
 
 
 def on_device(queries, keys, values, residual, out_weight):
@@ -309,14 +330,14 @@
     values2 = lax.ppermute(two, "ctx", ring2)
     back8 = lax.ppermute(both, "ctx", up)
     values1 = lax.ppermute(one, "ctx", ring1)
-    *state, weight = attend_own(q, k, v, out_weight)
-    state = attend_middle(q, k, [(keys4, values4)], (4,), state)
-    attended, sent = attend_last(
-        q, k, [(keys1, values1), (keys2, values2), back8], (1, 2, 8), state, weight
+    *state, low = attend_part(
+        q, k, [(k, v), (keys4, values4)], (0, 4), (), out_weight, 0
     )
+    *state, high = attend_part(q, k, [(keys2, values2)], (2,), state, out_weight, 1)
+    attended, sent = attend_last(q, k, [(keys1, values1), back8], (1, 8), state, (low, high))
     received = lax.ppermute(sent, "hid", [(0, 1), (1, 0)])
-    kept = project_kept(attended, weight, residual)
-    return (kept + received.astype(F32)).astype(BF16)
+    kept = project_kept(attended, (low, high), residual)
+    return added(kept, received)
 
 
 def solution(mesh):

time: 68.5 us -> 64 us (0.934)
  the two profiles are of different devices: /device:TPU:249 before, /device:TPU:251 now
where the time goes in v3:
time: 64 us; the launch traced here: 63.6 us
  starting transfers between devices  31.3 us (49%)
  Pallas kernels  18 us (28%)
  waiting for transfers between devices  14.2 us (22%)
    ppermute x1, starting transfers between devices, on_device(): back8 = lax.ppermute(both, 'ctx', up)  7.32 us
    pallas_call x2, Pallas kernels, attend_part(): pl.pallas_call(functools.partial(part_kernel, distances, bool(state), hal...  6.8 us
    pallas_call x1, Pallas kernels, attend_last(): pl.pallas_call(functools.partial(last_kernel, distances, stacked), out_sh...  5.82 us
    ppermute x1, waiting for transfers between devices, on_device(): values4 = lax.ppermute(values, 'ctx', up)  5.62 us
    ppermute x1, waiting for transfers between devices, on_device(): values1 = lax.ppermute(one, 'ctx', ring1)  5.62 us
    ppermute x1, starting transfers between devices, on_device(): keys4 = lax.ppermute(keys, 'ctx', up)  4.53 us
    ppermute x1, starting transfers between devices, on_device(): values2 = lax.ppermute(two, 'ctx', ring2)  3.75 us
    ppermute x1, starting transfers between devices, on_device(): received = lax.ppermute(sent, 'hid', [(0, 1), (1, 0)])  3.46 us
  transfers between devices with their start and end apart: 8, of which 4 were waited for; matrix products, arithmetic and copies ran while one was open for 0% of the time, Pallas kernels for 17%

profile of v3, /device:TPU:251, one launch (start us, length us, event | category | flops | bytes accessed | tf_op | source)
XLA Modules:
  0.0 63.6 jit_solution(8098469336336821046)
XLA Ops:
  0.0 0.0 copy-start.1
  0.0 4.5 %collective-permute-start.1 = (bf16[256,512]{1,0:T(8,128)(2,1)}, bf16[256,512]{1,0:T(8,128)(2,1)S(1)}, u32[]{:S(2)}, u32[]{:S(2)}) collective-permute-start(bf16[256,512]{1,0:T(8,128)(2,1)} %refs_1_.1), channel_id=1, source_target_pairs={{0,8},{2,10},{4,12},{6,14},{8,16},{10,18},{12,20},{14,22},{16,24},... | collective-permute-start | bytes 786440 | tf_op jit(solution)/shard_map/ppermute | solution.py:323
  4.5 3.2 %collective-permute-start.2 = (bf16[256,512]{1,0:T(8,128)(2,1)}, bf16[256,512]{1,0:T(8,128)(2,1)S(1)}, u32[]{:S(2)}, u32[]{:S(2)}) collective-permute-start(bf16[256,512]{1,0:T(8,128)(2,1)} %refs_2_.1), channel_id=1, source_target_pairs={{0,8},{2,10},{4,12},{6,14},{8,16},{10,18},{12,20},{14,22},{16,24},... | collective-permute-start | bytes 786440 | tf_op jit(solution)/shard_map/ppermute | solution.py:324
  7.8 1.4 %shard_map.55 = (bf16[256,2048]{1,0:T(8,128)(2,1)S(1)}, bf16[256,512]{1,0:T(8,128)(2,1)S(1)}, bf16[256,512]{1,0:T(8,128)(2,1)S(1)}) custom-call(bf16[256,2048]{1,0:T(8,128)(2,1)} %refs_0_.1, bf16[256,512]{1,0:T(8,128)(2,1)} %refs_1_.1, bf16[256,512]{1,0:T(8,128)(2,1)} %refs_2_.1), custom_call_target="tpu_custom_call" | custom-call | tf_op jit(solution)/shard_map/pallas_call | solution.py:204
  9.1 0.7 %collective-permute-done.1.back_keys_ref.back_ref.refs_2_ = bf16[256,512]{1,0:T(8,128)(2,1)S(1)} collective-permute-done((bf16[256,512]{1,0:T(8,128)(2,1)}, bf16[256,512]{1,0:T(8,128)(2,1)S(1)}, u32[]{:S(2)}, u32[]{:S(2)}) %collective-permute-start.1) | collective-permute-done | bytes 262176 | tf_op jit(solution)/shard_map/ppermute | solution.py:323
  9.8 5.6 %collective-permute-done.2.back_ref.refs_3_ = bf16[256,512]{1,0:T(8,128)(2,1)S(1)} collective-permute-done((bf16[256,512]{1,0:T(8,128)(2,1)}, bf16[256,512]{1,0:T(8,128)(2,1)S(1)}, u32[]{:S(2)}, u32[]{:S(2)}) %collective-permute-start.2) | collective-permute-done | bytes 262176 | tf_op jit(solution)/shard_map/ppermute | solution.py:324
  15.4 0.1 shard_map.56
  15.5 7.3 %collective-permute-start.4 = (bf16[512,512]{1,0:T(8,128)(2,1)S(1)}, bf16[512,512]{1,0:T(8,128)(2,1)S(1)}, u32[]{:S(2)}, u32[]{:S(2)}) collective-permute-start(bf16[512,512]{1,0:T(8,128)(2,1)S(1)} %get-tuple-element.25), channel_id=1, source_target_pairs={{0,8},{2,10},{4,12},{6,14},{8,16},{10,18},{12,20},{14,22},{16,24},... | collective-permute-start | bytes 1572872 | tf_op jit(solution)/shard_map/ppermute | solution.py:331
  22.9 3.7 %collective-permute-start.6 = (bf16[256,512]{1,0:T(8,128)(2,1)S(1)}, bf16[256,512]{1,0:T(8,128)(2,1)S(1)}, u32[]{:S(2)}, u32[]{:S(2)}) collective-permute-start(bf16[256,512]{1,0:T(8,128)(2,1)S(1)} %get-tuple-element.26), channel_id=1, source_target_pairs={{0,4},{2,6},{4,0},{6,2},{8,12},{10,14},{12,8},{14,10},{16,20},{18,... | collective-permute-start | bytes 786440 | tf_op jit(solution)/shard_map/ppermute | solution.py:330
  26.7 3.0 %collective-permute-start.5 = (bf16[256,512]{1,0:T(8,128)(2,1)S(1)}, bf16[256,512]{1,0:T(8,128)(2,1)S(1)}, u32[]{:S(2)}, u32[]{:S(2)}) collective-permute-start(bf16[256,512]{1,0:T(8,128)(2,1)S(1)} %shard_map.57), channel_id=1, source_target_pairs={{0,4},{2,6},{4,0},{6,2},{8,12},{10,14},{12,8},{14,10},{16,20},{18,... | collective-permute-start | bytes 786440 | tf_op jit(solution)/shard_map/ppermute | solution.py:328
  29.7 0.0 copy-done.1
  29.7 3.1 %collective-permute-start = (bf16[256,512]{1,0:T(8,128)(2,1)S(1)}, bf16[256,512]{1,0:T(8,128)(2,1)S(1)}, u32[]{:S(2)}, u32[]{:S(2)}) collective-permute-start(bf16[256,512]{1,0:T(8,128)(2,1)S(1)} %copy-done.1), channel_id=1, source_target_pairs={{0,2},{2,4},{4,6},{6,8},{8,10},{10,12},{12,14},{14,16},{16,18},{18... | collective-permute-start | bytes 786440 | tf_op jit(solution)/shard_map/ppermute | solution.py:325
  32.8 2.8 %collective-permute-start.3 = (bf16[256,512]{1,0:T(8,128)(2,1)S(1)}, bf16[256,512]{1,0:T(8,128)(2,1)S(1)}, u32[]{:S(2)}, u32[]{:S(2)}) collective-permute-start(bf16[256,512]{1,0:T(8,128)(2,1)S(1)} %get-tuple-element.24), channel_id=1, source_target_pairs={{0,2},{2,4},{4,6},{6,0},{8,10},{10,12},{12,14},{14,8},{16,18},{18,... | collective-permute-start | bytes 786440 | tf_op jit(solution)/shard_map/ppermute | solution.py:332
  35.7 3.4 %shard_map.58 = (f32[256,2048]{1,0:T(8,128)S(1)}, f32[256,2048]{1,0:T(8,128)S(1)}, f32[256,2048]{1,0:T(8,128)S(1)}, bf16[1024,4096]{1,0:T(8,128)(2,1)S(1)}) custom-call(bf16[256,2048]{1,0:T(8,128)(2,1)S(1)} %get-tuple-element.21.q_ref, bf16[256,512]{1,0:T(8,128)(2,1)S(1)} %get-tuple-element.22.mine_ref.first_ref.refs_0_, ...), custom_call_target="tpu_custom_call" | custom-call | flops 1073741824 | bytes 2097152 | tf_op jit(solution)/shard_map/pallas_call | solution.py:261
  39.1 0.0 collective-permute-done.6.refs_1_
  39.1 0.0 collective-permute-done.5.refs_0_
  39.1 3.4 %shard_map.59 = (f32[256,2048]{1,0:T(8,128)S(1)}, f32[256,2048]{1,0:T(8,128)S(1)}, f32[256,2048]{1,0:T(8,128)S(1)}, bf16[1024,4096]{1,0:T(8,128)(2,1)S(1)}) custom-call(bf16[256,2048]{1,0:T(8,128)(2,1)S(1)} %get-tuple-element.21.q_ref, bf16[256,512]{1,0:T(8,128)(2,1)S(1)} %get-tuple-element.22.mine_ref.first_ref.refs_0_, ...), custom_call_target="tpu_custom_call" | custom-call | flops 536870912 | bytes 2097152 | tf_op jit(solution)/shard_map/pallas_call | solution.py:261
  42.5 2.2 %collective-permute-done.refs_0_ = bf16[256,512]{1,0:T(8,128)(2,1)S(1)} collective-permute-done((bf16[256,512]{1,0:T(8,128)(2,1)S(1)}, bf16[256,512]{1,0:T(8,128)(2,1)S(1)}, u32[]{:S(2)}, u32[]{:S(2)}) %collective-permute-start) | collective-permute-done | bytes 262176 | tf_op jit(solution)/shard_map/ppermute | solution.py:325
  44.7 5.6 %collective-permute-done.3.refs_1_ = bf16[256,512]{1,0:T(8,128)(2,1)S(1)} collective-permute-done((bf16[256,512]{1,0:T(8,128)(2,1)S(1)}, bf16[256,512]{1,0:T(8,128)(2,1)S(1)}, u32[]{:S(2)}, u32[]{:S(2)}) %collective-permute-start.3) | collective-permute-done | bytes 262176 | tf_op jit(solution)/shard_map/ppermute | solution.py:332
  50.3 0.0 collective-permute-done.4.refs_2_
  50.3 0.0 copy-start
  50.4 5.8 %shard_map.60 = (bf16[256,2048]{1,0:T(8,128)(2,1)S(1)}, bf16[256,2048]{1,0:T(8,128)(2,1)S(1)}) custom-call(bf16[256,2048]{1,0:T(8,128)(2,1)S(1)} %get-tuple-element.21.q_ref, bf16[256,512]{1,0:T(8,128)(2,1)S(1)} %get-tuple-element.22.mine_ref.first_ref.refs_0_, bf16[256,512]{1,0:T(8,128)(2,1)S(1)} %collective-permute-done.refs_0_, ...), custom_call_target="tpu_custom_call" | custom-call | flops 3221225472 | bytes 2097152 | tf_op jit(solution)/shard_map/pallas_call | solution.py:281
  56.2 3.5 %collective-permute-start.7 = (bf16[256,2048]{1,0:T(8,128)(2,1)S(1)}, bf16[256,2048]{1,0:T(8,128)(2,1)S(1)}, u32[]{:S(2)}, u32[]{:S(2)}) collective-permute-start(bf16[256,2048]{1,0:T(8,128)(2,1)S(1)} %get-tuple-element.36), channel_id=1, source_target_pairs={{0,1},{1,0},{2,3},{3,2},{4,5},{5,4},{6,7},{7,6},{8,9},{9,8},{10,11... | collective-permute-start | bytes 3145736 | tf_op jit(solution)/shard_map/ppermute | solution.py:338
  59.6 0.0 copy-done
  59.7 2.9 %shard_map.61.kept_ref = f32[256,2048]{1,0:T(8,128)S(1)} custom-call(bf16[256,2048]{1,0:T(8,128)(2,1)S(1)} %get-tuple-element.35.att_ref, bf16[1024,4096]{1,0:T(8,128)(2,1)S(1)} %get-tuple-element.33.refs_6_.low_ref, bf16[1024,4096]{1,0:T(8,128)(2,1)S(1)} %get-tuple-element.34.refs_7_.high_ref, bf16[256,2048]{1,0:T(8,128)(2,1)S(1)} %copy-done), custom_call_target="tpu_custom_call" | custom-call | flops 2147483648 | bytes 2097152 | tf_op jit(solution)/shard_map/pallas_call | solution.py:293
  62.5 0.0 collective-permute-done.7.got_ref
  62.5 1.0 %shard_map.62 = bf16[256,2048]{1,0:T(8,128)(2,1)} custom-call(f32[256,2048]{1,0:T(8,128)S(1)} %shard_map.61.kept_ref, bf16[256,2048]{1,0:T(8,128)(2,1)S(1)} %collective-permute-done.7.got_ref), custom_call_target="tpu_custom_call" | custom-call | tf_op jit(solution)/shard_map/pallas_call | solution.py:306
  (1 shorter events, 0.0 us)
Async XLA Ops:
  0.0 29.7 %copy-start.1 = (bf16[256,512]{1,0:T(8,128)(2,1)S(1)}, bf16[256,512]{1,0:T(8,128)(2,1)}, u32[]{:S(2)}) copy-start(bf16[256,512]{1,0:T(8,128)(2,1)} %refs_1_.1) | copy-start | bytes 786436
  0.0 9.8 %collective-permute-start.1 = (bf16[256,512]{1,0:T(8,128)(2,1)}, bf16[256,512]{1,0:T(8,128)(2,1)S(1)}, u32[]{:S(2)}, u32[]{:S(2)}) collective-permute-start(bf16[256,512]{1,0:T(8,128)(2,1)} %refs_1_.1), channel_id=1, source_target_pairs={{0,8},{2,10},{4,12},{6,14},{8,16},{10,18},{12,20},{14,22},{16,24},... | collective-permute-start | bytes 786440 | tf_op jit(solution)/shard_map/ppermute | solution.py:323
  4.5 10.9 %collective-permute-start.2 = (bf16[256,512]{1,0:T(8,128)(2,1)}, bf16[256,512]{1,0:T(8,128)(2,1)S(1)}, u32[]{:S(2)}, u32[]{:S(2)}) collective-permute-start(bf16[256,512]{1,0:T(8,128)(2,1)} %refs_2_.1), channel_id=1, source_target_pairs={{0,8},{2,10},{4,12},{6,14},{8,16},{10,18},{12,20},{14,22},{16,24},... | collective-permute-start | bytes 786440 | tf_op jit(solution)/shard_map/ppermute | solution.py:324
  15.5 34.8 %collective-permute-start.4 = (bf16[512,512]{1,0:T(8,128)(2,1)S(1)}, bf16[512,512]{1,0:T(8,128)(2,1)S(1)}, u32[]{:S(2)}, u32[]{:S(2)}) collective-permute-start(bf16[512,512]{1,0:T(8,128)(2,1)S(1)} %get-tuple-element.25), channel_id=1, source_target_pairs={{0,8},{2,10},{4,12},{6,14},{8,16},{10,18},{12,20},{14,22},{16,24},... | collective-permute-start | bytes 1572872 | tf_op jit(solution)/shard_map/ppermute | solution.py:331
  22.9 16.2 %collective-permute-start.6 = (bf16[256,512]{1,0:T(8,128)(2,1)S(1)}, bf16[256,512]{1,0:T(8,128)(2,1)S(1)}, u32[]{:S(2)}, u32[]{:S(2)}) collective-permute-start(bf16[256,512]{1,0:T(8,128)(2,1)S(1)} %get-tuple-element.26), channel_id=1, source_target_pairs={{0,4},{2,6},{4,0},{6,2},{8,12},{10,14},{12,8},{14,10},{16,20},{18,... | collective-permute-start | bytes 786440 | tf_op jit(solution)/shard_map/ppermute | solution.py:330
  26.7 12.4 %collective-permute-start.5 = (bf16[256,512]{1,0:T(8,128)(2,1)S(1)}, bf16[256,512]{1,0:T(8,128)(2,1)S(1)}, u32[]{:S(2)}, u32[]{:S(2)}) collective-permute-start(bf16[256,512]{1,0:T(8,128)(2,1)S(1)} %shard_map.57), channel_id=1, source_target_pairs={{0,4},{2,6},{4,0},{6,2},{8,12},{10,14},{12,8},{14,10},{16,20},{18,... | collective-permute-start | bytes 786440 | tf_op jit(solution)/shard_map/ppermute | solution.py:328
  29.7 15.0 %collective-permute-start = (bf16[256,512]{1,0:T(8,128)(2,1)S(1)}, bf16[256,512]{1,0:T(8,128)(2,1)S(1)}, u32[]{:S(2)}, u32[]{:S(2)}) collective-permute-start(bf16[256,512]{1,0:T(8,128)(2,1)S(1)} %copy-done.1), channel_id=1, source_target_pairs={{0,2},{2,4},{4,6},{6,8},{8,10},{10,12},{12,14},{14,16},{16,18},{18... | collective-permute-start | bytes 786440 | tf_op jit(solution)/shard_map/ppermute | solution.py:325
  32.8 17.5 %collective-permute-start.3 = (bf16[256,512]{1,0:T(8,128)(2,1)S(1)}, bf16[256,512]{1,0:T(8,128)(2,1)S(1)}, u32[]{:S(2)}, u32[]{:S(2)}) collective-permute-start(bf16[256,512]{1,0:T(8,128)(2,1)S(1)} %get-tuple-element.24), channel_id=1, source_target_pairs={{0,2},{2,4},{4,6},{6,0},{8,10},{10,12},{12,14},{14,8},{16,18},{18,... | collective-permute-start | bytes 786440 | tf_op jit(solution)/shard_map/ppermute | solution.py:332
  50.3 9.3 %copy-start = (bf16[256,2048]{1,0:T(8,128)(2,1)S(1)}, bf16[256,2048]{1,0:T(8,128)(2,1)}, u32[]{:S(2)}) copy-start(bf16[256,2048]{1,0:T(8,128)(2,1)} %res_ref.1) | copy-start | bytes 3145732
  56.2 6.4 %collective-permute-start.7 = (bf16[256,2048]{1,0:T(8,128)(2,1)S(1)}, bf16[256,2048]{1,0:T(8,128)(2,1)S(1)}, u32[]{:S(2)}, u32[]{:S(2)}) collective-permute-start(bf16[256,2048]{1,0:T(8,128)(2,1)S(1)} %get-tuple-element.36), channel_id=1, source_target_pairs={{0,1},{1,0},{2,3},{3,2},{4,5},{5,4},{6,7},{7,6},{8,9},{9,8},{10,11... | collective-permute-start | bytes 3145736 | tf_op jit(solution)/shard_map/ppermute | solution.py:338

commit v4 on v3

--- a/solution.py
+++ b/solution.py
@@ -138,18 +138,20 @@
 def last_kernel(distances, stacked, q_ref, first_ref, *refs):
     refs = list(refs)
     pairs = split_pairs(refs, stacked)
-    prev, (*weights, att_ref, send_ref) = refs[:3], refs[3:]
+    prev, (att_ref,) = refs[:3], refs[3:]
     for g in range(first_ref.shape[1] // HEAD):
         blocks = head_blocks(g, pairs, distances, first_ref)
         for where, (acc, _, l) in softmax_units(q_ref, g, blocks, prev):
             att_ref[where] = (acc / l).astype(BF16)
+
+
+def partner_kernel(att_ref, low_ref, high_ref, send_ref):
     width, tile = send_ref.shape[1], 512
     base = (1 - lax.axis_index("hid")) * width
 
-    @pl.loop(0, width // tile)
-    def _(t):
+    for t in range(width // tile):
         send_ref[:, columns(t * tile, tile)] = product(
-            att_ref, weights, columns(base + t * tile, tile)
+            att_ref, (low_ref, high_ref), columns(base + t * tile, tile)
         ).astype(BF16)
 
 
@@ -157,8 +159,7 @@
     width, tile = out_ref.shape[1], 512
     base = lax.axis_index("hid") * width
 
-    @pl.loop(0, width // tile)
-    def _(t):
+    for t in range(width // tile):
         here = columns(t * tile, tile)
         out_ref[:, here] = res_ref[:, here].astype(F32) + product(
             att_ref, (low_ref, high_ref), columns(base + t * tile, tile)
@@ -274,18 +275,30 @@
     return stacked, [a for s in sources for a in (s if isinstance(s, tuple) else (s,))]
 
 
-def attend_last(q, first, sources, distances, state, weights):
+def attend_last(q, first, sources, distances, state):
     stacked, arrays = flat(sources)
-    rows, width = q.shape
-    half = weights[0].shape[1] // 2
     return pl.pallas_call(
         functools.partial(last_kernel, distances, stacked),
-        out_shape=(pltpu.VMEM(q.shape, BF16), pltpu.VMEM((rows, half), BF16)),
-        in_specs=[WHOLE] * (7 + len(arrays)),
-        out_specs=(WHOLE,) * 2,
-        cost_estimate=estimate(rows, width, len(sources), 2 * rows * width * half),
+        out_shape=pltpu.VMEM(q.shape, BF16),
+        in_specs=[WHOLE] * (5 + len(arrays)),
+        out_specs=WHOLE,
+        cost_estimate=estimate(*q.shape, len(sources)),
         compiler_params=params(8),
-    )(q, first, *arrays, *state, *weights)
+    )(q, first, *arrays, *state)
+
+
+def project_partner(att, weights):
+    rows, half = att.shape[0], weights[0].shape[1] // 2
+    return pl.pallas_call(
+        partner_kernel,
+        out_shape=pltpu.VMEM((rows, half), BF16),
+        in_specs=[WHOLE] * 3,
+        out_specs=WHOLE,
+        cost_estimate=pl.CostEstimate(
+            flops=2 * rows * att.shape[1] * half, bytes_accessed=2 * MIB, transcendentals=0
+        ),
+        compiler_params=params(4),
+    )(att, *weights)
 
 
 def project_kept(att, weights, residual):
@@ -333,8 +346,9 @@
     *state, low = attend_part(
         q, k, [(k, v), (keys4, values4)], (0, 4), (), out_weight, 0
     )
-    *state, high = attend_part(q, k, [(keys2, values2)], (2,), state, out_weight, 1)
-    attended, sent = attend_last(q, k, [(keys1, values1), back8], (1, 8), state, (low, high))
+    *state, high = attend_part(q, k, [(keys1, values1)], (1,), state, out_weight, 1)
+    attended = attend_last(q, k, [(keys2, values2), back8], (2, 8), state)
+    sent = project_partner(attended, (low, high))
     received = lax.ppermute(sent, "hid", [(0, 1), (1, 0)])
     kept = project_kept(attended, (low, high), residual)
     return added(kept, received)

time: 64 us -> 69.1 us (1.080)
  the two profiles are of different devices: /device:TPU:251 before, /device:TPU:249 now
where the time goes in v4:
time: 69.1 us; the launch traced here: 68.7 us
  starting transfers between devices  31.7 us (46%)
  waiting for transfers between devices  19.8 us (29%)
  Pallas kernels  17 us (25%)
    ppermute x1, waiting for transfers between devices, on_device(): values1 = lax.ppermute(one, 'ctx', ring1)  13.5 us
    ppermute x1, starting transfers between devices, on_device(): back8 = lax.ppermute(both, 'ctx', up)  7.32 us
    pallas_call x2, Pallas kernels, attend_part(): pl.pallas_call(functools.partial(part_kernel, distances, bool(state), hal...  6.79 us
    ppermute x1, waiting for transfers between devices, on_device(): keys4 = lax.ppermute(keys, 'ctx', up)  5.62 us
    ppermute x1, starting transfers between devices, on_device(): values4 = lax.ppermute(values, 'ctx', up)  4.53 us
    ppermute x1, starting transfers between devices, on_device(): values2 = lax.ppermute(two, 'ctx', ring2)  3.63 us
    ppermute x1, starting transfers between devices, on_device(): received = lax.ppermute(sent, 'hid', [(0, 1), (1, 0)])  3.58 us
    ppermute x1, starting transfers between devices, on_device(): keys4 = lax.ppermute(keys, 'ctx', up)  3.2 us
  transfers between devices with their start and end apart: 8, of which 3 were waited for; matrix products, arithmetic and copies ran while one was open for 0% of the time, Pallas kernels for 15%

profile of v4, /device:TPU:249, one launch (start us, length us, event | category | flops | bytes accessed | tf_op | source)
XLA Modules:
  0.0 68.7 jit_solution(1035037752381399830)
XLA Ops:
  0.0 0.0 copy-start.1
  0.0 4.5 %collective-permute-start.2 = (bf16[256,512]{1,0:T(8,128)(2,1)}, bf16[256,512]{1,0:T(8,128)(2,1)S(1)}, u32[]{:S(2)}, u32[]{:S(2)}) collective-permute-start(bf16[256,512]{1,0:T(8,128)(2,1)} %refs_2_.1), channel_id=1, source_target_pairs={{0,8},{2,10},{4,12},{6,14},{8,16},{10,18},{12,20},{14,22},{16,24},... | collective-permute-start | bytes 786440 | tf_op jit(solution)/shard_map/ppermute | solution.py:337
  4.5 3.2 %collective-permute-start = (bf16[256,512]{1,0:T(8,128)(2,1)}, bf16[256,512]{1,0:T(8,128)(2,1)S(1)}, u32[]{:S(2)}, u32[]{:S(2)}) collective-permute-start(bf16[256,512]{1,0:T(8,128)(2,1)} %refs_1_.1), channel_id=1, source_target_pairs={{0,8},{2,10},{4,12},{6,14},{8,16},{10,18},{12,20},{14,22},{16,24},... | collective-permute-start | bytes 786440 | tf_op jit(solution)/shard_map/ppermute | solution.py:336
  7.8 1.4 %shard_map.55 = (bf16[256,2048]{1,0:T(8,128)(2,1)S(1)}, bf16[256,512]{1,0:T(8,128)(2,1)S(1)}, bf16[256,512]{1,0:T(8,128)(2,1)S(1)}) custom-call(bf16[256,2048]{1,0:T(8,128)(2,1)} %refs_0_.1, bf16[256,512]{1,0:T(8,128)(2,1)} %refs_1_.1, bf16[256,512]{1,0:T(8,128)(2,1)} %refs_2_.1), custom_call_target="tpu_custom_call" | custom-call | tf_op jit(solution)/shard_map/pallas_call | solution.py:205
  9.1 0.7 %collective-permute-done.2.back_ref.refs_3_ = bf16[256,512]{1,0:T(8,128)(2,1)S(1)} collective-permute-done((bf16[256,512]{1,0:T(8,128)(2,1)}, bf16[256,512]{1,0:T(8,128)(2,1)S(1)}, u32[]{:S(2)}, u32[]{:S(2)}) %collective-permute-start.2) | collective-permute-done | bytes 262176 | tf_op jit(solution)/shard_map/ppermute | solution.py:337
  9.8 5.6 %collective-permute-done.back_ref.back_keys_ref.refs_2_ = bf16[256,512]{1,0:T(8,128)(2,1)S(1)} collective-permute-done((bf16[256,512]{1,0:T(8,128)(2,1)}, bf16[256,512]{1,0:T(8,128)(2,1)S(1)}, u32[]{:S(2)}, u32[]{:S(2)}) %collective-permute-start) | collective-permute-done | bytes 262176 | tf_op jit(solution)/shard_map/ppermute | solution.py:336
  15.4 0.1 shard_map.57
  15.5 7.3 %collective-permute-start.4 = (bf16[512,512]{1,0:T(8,128)(2,1)S(1)}, bf16[512,512]{1,0:T(8,128)(2,1)S(1)}, u32[]{:S(2)}, u32[]{:S(2)}) collective-permute-start(bf16[512,512]{1,0:T(8,128)(2,1)S(1)} %get-tuple-element.23), channel_id=1, source_target_pairs={{0,8},{2,10},{4,12},{6,14},{8,16},{10,18},{12,20},{14,22},{16,24},... | collective-permute-start | bytes 1572872 | tf_op jit(solution)/shard_map/ppermute | solution.py:344
  22.9 0.0 copy-done.1
  22.9 3.1 %collective-permute-start.5 = (bf16[256,512]{1,0:T(8,128)(2,1)S(1)}, bf16[256,512]{1,0:T(8,128)(2,1)S(1)}, u32[]{:S(2)}, u32[]{:S(2)}) collective-permute-start(bf16[256,512]{1,0:T(8,128)(2,1)S(1)} %copy-done.1), channel_id=1, source_target_pairs={{0,2},{2,4},{4,6},{6,8},{8,10},{10,12},{12,14},{14,16},{16,18},{18... | collective-permute-start | bytes 786440 | tf_op jit(solution)/shard_map/ppermute | solution.py:338
  26.0 3.1 %collective-permute-start.6 = (bf16[256,512]{1,0:T(8,128)(2,1)S(1)}, bf16[256,512]{1,0:T(8,128)(2,1)S(1)}, u32[]{:S(2)}, u32[]{:S(2)}) collective-permute-start(bf16[256,512]{1,0:T(8,128)(2,1)S(1)} %get-tuple-element.24), channel_id=1, source_target_pairs={{0,2},{2,4},{4,6},{6,0},{8,10},{10,12},{12,14},{14,8},{16,18},{18,... | collective-permute-start | bytes 786440 | tf_op jit(solution)/shard_map/ppermute | solution.py:345
  29.2 3.2 %collective-permute-start.1 = (bf16[256,512]{1,0:T(8,128)(2,1)S(1)}, bf16[256,512]{1,0:T(8,128)(2,1)S(1)}, u32[]{:S(2)}, u32[]{:S(2)}) collective-permute-start(bf16[256,512]{1,0:T(8,128)(2,1)S(1)} %shard_map.56), channel_id=1, source_target_pairs={{0,4},{2,6},{4,0},{6,2},{8,12},{10,14},{12,8},{14,10},{16,20},{18,... | collective-permute-start | bytes 786440 | tf_op jit(solution)/shard_map/ppermute | solution.py:341
  32.3 3.6 %collective-permute-start.3 = (bf16[256,512]{1,0:T(8,128)(2,1)S(1)}, bf16[256,512]{1,0:T(8,128)(2,1)S(1)}, u32[]{:S(2)}, u32[]{:S(2)}) collective-permute-start(bf16[256,512]{1,0:T(8,128)(2,1)S(1)} %get-tuple-element.22), channel_id=1, source_target_pairs={{0,4},{2,6},{4,0},{6,2},{8,12},{10,14},{12,8},{14,10},{16,20},{18,... | collective-permute-start | bytes 786440 | tf_op jit(solution)/shard_map/ppermute | solution.py:343
  36.0 3.4 %shard_map.58 = (f32[256,2048]{1,0:T(8,128)S(1)}, f32[256,2048]{1,0:T(8,128)S(1)}, f32[256,2048]{1,0:T(8,128)S(1)}, bf16[1024,4096]{1,0:T(8,128)(2,1)S(1)}) custom-call(bf16[256,2048]{1,0:T(8,128)(2,1)S(1)} %get-tuple-element.19.q_ref, bf16[256,512]{1,0:T(8,128)(2,1)S(1)} %get-tuple-element.20.mine_ref.first_ref.refs_0_, ...), custom_call_target="tpu_custom_call" | custom-call | flops 1073741824 | bytes 2097152 | tf_op jit(solution)/shard_map/pallas_call | solution.py:262
  39.4 0.0 collective-permute-done.5.refs_0_
  39.4 13.5 %collective-permute-done.6.refs_1_ = bf16[256,512]{1,0:T(8,128)(2,1)S(1)} collective-permute-done((bf16[256,512]{1,0:T(8,128)(2,1)S(1)}, bf16[256,512]{1,0:T(8,128)(2,1)S(1)}, u32[]{:S(2)}, u32[]{:S(2)}) %collective-permute-start.6) | collective-permute-done | bytes 262176 | tf_op jit(solution)/shard_map/ppermute | solution.py:345
  52.9 3.4 %shard_map.59 = (f32[256,2048]{1,0:T(8,128)S(1)}, f32[256,2048]{1,0:T(8,128)S(1)}, f32[256,2048]{1,0:T(8,128)S(1)}, bf16[1024,4096]{1,0:T(8,128)(2,1)S(1)}) custom-call(bf16[256,2048]{1,0:T(8,128)(2,1)S(1)} %get-tuple-element.19.q_ref, bf16[256,512]{1,0:T(8,128)(2,1)S(1)} %get-tuple-element.20.mine_ref.first_ref.refs_0_, ...), custom_call_target="tpu_custom_call" | custom-call | flops 536870912 | bytes 2097152 | tf_op jit(solution)/shard_map/pallas_call | solution.py:262
  56.3 0.0 collective-permute-done.1.refs_0_
  56.3 0.0 collective-permute-done.3.refs_1_
  56.3 0.0 collective-permute-done.4.refs_2_
  56.3 3.0 %shard_map.60.att_ref = bf16[256,2048]{1,0:T(8,128)(2,1)S(1)} custom-call(bf16[256,2048]{1,0:T(8,128)(2,1)S(1)} %get-tuple-element.19.q_ref, bf16[256,512]{1,0:T(8,128)(2,1)S(1)} %get-tuple-element.20.mine_ref.first_ref.refs_0_, bf16[256,512]{1,0:T(8,128)(2,1)S(1)} %collective-permute-done.1.refs_0_, bf16[256,512]{1,0:T(8,128)(2,1)S(1)} %collective-permute-done.3.refs_1_, ...), custom_call_target="tpu_custom_call" | custom-call | flops 1073741824 | bytes 2097152 | tf_op jit(solution)/shard_map/pallas_call | solution.py:280
  59.3 0.0 copy-start
  59.3 2.4 %shard_map.62 = bf16[256,2048]{1,0:T(8,128)(2,1)S(1)} custom-call(bf16[256,2048]{1,0:T(8,128)(2,1)S(1)} %shard_map.60.att_ref, bf16[1024,4096]{1,0:T(8,128)(2,1)S(1)} %get-tuple-element.31.low_ref, bf16[1024,4096]{1,0:T(8,128)(2,1)S(1)} %get-tuple-element.32.high_ref), custom_call_target="tpu_custom_call" | custom-call | flops 2147483648 | bytes 2097152 | tf_op jit(solution)/shard_map/pallas_call | solution.py:292
  61.7 3.6 %collective-permute-start.7 = (bf16[256,2048]{1,0:T(8,128)(2,1)S(1)}, bf16[256,2048]{1,0:T(8,128)(2,1)S(1)}, u32[]{:S(2)}, u32[]{:S(2)}) collective-permute-start(bf16[256,2048]{1,0:T(8,128)(2,1)S(1)} %shard_map.62), channel_id=1, source_target_pairs={{0,1},{1,0},{2,3},{3,2},{4,5},{5,4},{6,7},{7,6},{8,9},{9,8},{10,11... | collective-permute-start | bytes 3145736 | tf_op jit(solution)/shard_map/ppermute | solution.py:352
  65.3 0.0 copy-done
  65.3 2.4 %shard_map.61.kept_ref = f32[256,2048]{1,0:T(8,128)S(1)} custom-call(bf16[256,2048]{1,0:T(8,128)(2,1)S(1)} %shard_map.60.att_ref, bf16[1024,4096]{1,0:T(8,128)(2,1)S(1)} %get-tuple-element.31.low_ref, bf16[1024,4096]{1,0:T(8,128)(2,1)S(1)} %get-tuple-element.32.high_ref, bf16[256,2048]{1,0:T(8,128)(2,1)S(1)} %copy-done), custom_call_target="tpu_custom_call" | custom-call | flops 2147483648 | bytes 2097152 | tf_op jit(solution)/shard_map/pallas_call | solution.py:306
  67.6 0.0 collective-permute-done.7.got_ref
  67.7 1.0 %shard_map.63 = bf16[256,2048]{1,0:T(8,128)(2,1)} custom-call(f32[256,2048]{1,0:T(8,128)S(1)} %shard_map.61.kept_ref, bf16[256,2048]{1,0:T(8,128)(2,1)S(1)} %collective-permute-done.7.got_ref), custom_call_target="tpu_custom_call" | custom-call | tf_op jit(solution)/shard_map/pallas_call | solution.py:319
  (1 shorter events, 0.0 us)
Async XLA Ops:
  0.0 22.9 %copy-start.1 = (bf16[256,512]{1,0:T(8,128)(2,1)S(1)}, bf16[256,512]{1,0:T(8,128)(2,1)}, u32[]{:S(2)}) copy-start(bf16[256,512]{1,0:T(8,128)(2,1)} %refs_1_.1) | copy-start | bytes 786436
  0.0 9.8 %collective-permute-start.2 = (bf16[256,512]{1,0:T(8,128)(2,1)}, bf16[256,512]{1,0:T(8,128)(2,1)S(1)}, u32[]{:S(2)}, u32[]{:S(2)}) collective-permute-start(bf16[256,512]{1,0:T(8,128)(2,1)} %refs_2_.1), channel_id=1, source_target_pairs={{0,8},{2,10},{4,12},{6,14},{8,16},{10,18},{12,20},{14,22},{16,24},... | collective-permute-start | bytes 786440 | tf_op jit(solution)/shard_map/ppermute | solution.py:337
  4.5 10.9 %collective-permute-start = (bf16[256,512]{1,0:T(8,128)(2,1)}, bf16[256,512]{1,0:T(8,128)(2,1)S(1)}, u32[]{:S(2)}, u32[]{:S(2)}) collective-permute-start(bf16[256,512]{1,0:T(8,128)(2,1)} %refs_1_.1), channel_id=1, source_target_pairs={{0,8},{2,10},{4,12},{6,14},{8,16},{10,18},{12,20},{14,22},{16,24},... | collective-permute-start | bytes 786440 | tf_op jit(solution)/shard_map/ppermute | solution.py:336
  15.5 40.8 %collective-permute-start.4 = (bf16[512,512]{1,0:T(8,128)(2,1)S(1)}, bf16[512,512]{1,0:T(8,128)(2,1)S(1)}, u32[]{:S(2)}, u32[]{:S(2)}) collective-permute-start(bf16[512,512]{1,0:T(8,128)(2,1)S(1)} %get-tuple-element.23), channel_id=1, source_target_pairs={{0,8},{2,10},{4,12},{6,14},{8,16},{10,18},{12,20},{14,22},{16,24},... | collective-permute-start | bytes 1572872 | tf_op jit(solution)/shard_map/ppermute | solution.py:344
  22.9 16.5 %collective-permute-start.5 = (bf16[256,512]{1,0:T(8,128)(2,1)S(1)}, bf16[256,512]{1,0:T(8,128)(2,1)S(1)}, u32[]{:S(2)}, u32[]{:S(2)}) collective-permute-start(bf16[256,512]{1,0:T(8,128)(2,1)S(1)} %copy-done.1), channel_id=1, source_target_pairs={{0,2},{2,4},{4,6},{6,8},{8,10},{10,12},{12,14},{14,16},{16,18},{18... | collective-permute-start | bytes 786440 | tf_op jit(solution)/shard_map/ppermute | solution.py:338
  26.0 26.9 %collective-permute-start.6 = (bf16[256,512]{1,0:T(8,128)(2,1)S(1)}, bf16[256,512]{1,0:T(8,128)(2,1)S(1)}, u32[]{:S(2)}, u32[]{:S(2)}) collective-permute-start(bf16[256,512]{1,0:T(8,128)(2,1)S(1)} %get-tuple-element.24), channel_id=1, source_target_pairs={{0,2},{2,4},{4,6},{6,0},{8,10},{10,12},{12,14},{14,8},{16,18},{18,... | collective-permute-start | bytes 786440 | tf_op jit(solution)/shard_map/ppermute | solution.py:345
  29.2 27.1 %collective-permute-start.1 = (bf16[256,512]{1,0:T(8,128)(2,1)S(1)}, bf16[256,512]{1,0:T(8,128)(2,1)S(1)}, u32[]{:S(2)}, u32[]{:S(2)}) collective-permute-start(bf16[256,512]{1,0:T(8,128)(2,1)S(1)} %shard_map.56), channel_id=1, source_target_pairs={{0,4},{2,6},{4,0},{6,2},{8,12},{10,14},{12,8},{14,10},{16,20},{18,... | collective-permute-start | bytes 786440 | tf_op jit(solution)/shard_map/ppermute | solution.py:341
  32.3 24.0 %collective-permute-start.3 = (bf16[256,512]{1,0:T(8,128)(2,1)S(1)}, bf16[256,512]{1,0:T(8,128)(2,1)S(1)}, u32[]{:S(2)}, u32[]{:S(2)}) collective-permute-start(bf16[256,512]{1,0:T(8,128)(2,1)S(1)} %get-tuple-element.22), channel_id=1, source_target_pairs={{0,4},{2,6},{4,0},{6,2},{8,12},{10,14},{12,8},{14,10},{16,20},{18,... | collective-permute-start | bytes 786440 | tf_op jit(solution)/shard_map/ppermute | solution.py:343
  59.3 6.0 %copy-start = (bf16[256,2048]{1,0:T(8,128)(2,1)S(1)}, bf16[256,2048]{1,0:T(8,128)(2,1)}, u32[]{:S(2)}) copy-start(bf16[256,2048]{1,0:T(8,128)(2,1)} %res_ref.1) | copy-start | bytes 3145732
  61.7 6.0 %collective-permute-start.7 = (bf16[256,2048]{1,0:T(8,128)(2,1)S(1)}, bf16[256,2048]{1,0:T(8,128)(2,1)S(1)}, u32[]{:S(2)}, u32[]{:S(2)}) collective-permute-start(bf16[256,2048]{1,0:T(8,128)(2,1)S(1)} %shard_map.62), channel_id=1, source_target_pairs={{0,1},{1,0},{2,3},{3,2},{4,5},{5,4},{6,7},{7,6},{8,9},{9,8},{10,11... | collective-permute-start | bytes 3145736 | tf_op jit(solution)/shard_map/ppermute | solution.py:352
